TPU v7x, 128 devices: a whole 4x4x4 slice. The times are simulated.
128 devices in a mesh: gx: 8 (over y, core), gy: 16 (over z, x).
Axes of the slice: x: 4, y: 4, z: 4, core: 2. Of those that a mesh axis runs over, the one named last changes fastest.
Arguments:
- positions: float32 [3, 2048, 8192], P(None, 'gx', 'gy'), may hold values from -6 to 6
- velocity: float32 [3, 2048, 8192], P(None, 'gx', 'gy'), may hold values from -3 to 3
- stiffness: float32 [2048, 8192], P('gx', 'gy'), may hold values from 0.5 to 4
- send_tiles: int32 [8, 16, 512], P('gx', 'gy'), may hold values from -1 to 1023, as said below
- pair_tiles: int32 [8, 16, 2, 256], P('gx', 'gy'), may hold values from -1 to 511, as said below
Outputs:
- new_positions: float32 [3, 2048, 8192], P(None, 'gx', 'gy')
- new_velocity: float32 [3, 2048, 8192], P(None, 'gx', 'gy')
Inputs may be any that keep to these rules, and one draw needn't show every extreme that they name: `send_tiles`: entry o * 4 + k of a device names the patch tile in slot k towards owner o, -1 marking an empty slot; the filled slots towards an owner come first, and some owner receives all 4 slots filled from every device. `pair_tiles`: at each owner, column m is a face-pair tile: its two rows name two different filled received slots, slot s * 4 + k being slot k sent to this owner by owner s. Unused columns hold -1 in both rows and follow the used ones; some owner uses all 256 columns.
All inputs are finite; a program needn't handle non-finite values.
Results may differ from a plain program's by a relative error of at most 0.0003.
Values sent between devices are 32-bit elements; how exact they have to be, the bound alone decides.
No kernel may reach another device: no remote copies, remote signals or barrier semaphores. Data moves between devices by JAX's collectives and lax.ppermute only.
A program may use at most 64 MiB of HBM per device.

v0:
```python
import functools
import math

import jax
import jax.numpy as jnp
from jax import lax
from jax.experimental import pallas as pl
from jax.experimental.pallas import tpu as pltpu
from jax.sharding import PartitionSpec as P

TILE = 128
STEPS = 2
SLOTS = 4
GROUP = 8

time_step = 0.1
damping = 0.2
hardening = 0.1
bend_gain = 0.02
contact_gain = 0.25
inverse_width = 0.5

BF = jnp.bfloat16
F32 = jnp.float32

SCALE = math.sqrt(2.0 * inverse_width * math.log2(math.e))
GAIN_LOG = math.log2(contact_gain)
NORM_SHIFT = (GAIN_LOG - 1.0) / 2.0

VMEM = pl.BlockSpec(memory_space=pltpu.VMEM)
SMEM = pl.BlockSpec(memory_space=pltpu.SMEM)


def tile_row(route, slot, rows, blocks):
    tile = jnp.maximum(route[slot], 0)
    return lax.rem(tile, blocks) * rows + lax.div(tile, blocks)


def pack_tiles(route, held, sent, rows):
    blocks = held.shape[1] // rows

    def body(step, carry):
        for u in range(8):
            slot = step * 8 + u
            row = tile_row(route, slot, rows, blocks)
            for c in range(3):
                sent[pl.ds(slot * 3 + c, 1), :] = held[c, pl.ds(row, 1), :]
        return carry

    lax.fori_loop(0, route.shape[0] // 8, body, 0)


def pack_edges(x, cols, rows_out, rows, columns):
    lane = lax.broadcasted_iota(jnp.int32, (rows, TILE), 1)
    mixed = jnp.zeros((rows, TILE), F32)
    for c in range(3):
        head = x[c, :, 0:TILE]
        tail = x[c, :, columns - TILE : columns]
        if c:
            head = pltpu.roll(head, 4 * c, axis=1)
        tail = pltpu.roll(tail, 4 * c + 4, axis=1)
        mixed = jnp.where((lane == 4 * c) | (lane == 4 * c + 1), head, mixed)
        mixed = jnp.where((lane == 4 * c + 2) | (lane == 4 * c + 3), tail, mixed)
    cols[...] = jnp.transpose(mixed)[0:16, :]
    for c in range(3):
        rows_out[4 * c : 4 * c + 2, :] = x[c, 0:2, :]
        rows_out[4 * c + 2 : 4 * c + 4, :] = x[c, rows - 2 : rows, :]
    rows_out[12:16, :] = jnp.zeros((4, columns), F32)


def pack_kernel(route, x, sent, cols, rows_out, held):
    rows = x.shape[1]
    for c in range(3):
        for b in range(x.shape[2] // TILE):
            held[c, b * rows : (b + 1) * rows, :] = x[c, :, b * TILE : (b + 1) * TILE]
    pack_tiles(route, held, sent, rows)
    pack_edges(x, cols, rows_out, x.shape[1], x.shape[2])


def blocked(shape):
    return (shape[0], shape[1] * shape[2] // TILE, TILE)


def packed_shapes(route, x):
    _, rows, columns = x.shape
    return (
        jax.ShapeDtypeStruct((route.shape[0] * 3, TILE), F32),
        jax.ShapeDtypeStruct((16, rows), F32),
        jax.ShapeDtypeStruct((16, columns), F32),
    )


def pack(route, x):
    return pl.pallas_call(
        pack_kernel,
        out_shape=packed_shapes(route, x),
        in_specs=[SMEM, VMEM],
        out_specs=(VMEM, VMEM, VMEM),
        scratch_shapes=[pltpu.VMEM(blocked(x.shape), F32)],
        name="pack",
        cost_estimate=pl.CostEstimate(flops=400_000, bytes_accessed=3_000_000, transcendentals=0),
    )(route, x)


def stencil_kernel(flags, x, velocity, stiffness, left, right, above, below, base, wide, curve):
    _, rows, columns = x.shape
    full = columns + 2 * TILE
    tail = TILE + columns
    turned_left = jnp.transpose(jnp.concatenate([left[...], jnp.zeros((TILE - 16, rows), F32)], axis=0))
    turned_right = jnp.transpose(jnp.concatenate([right[...], jnp.zeros((TILE - 16, rows), F32)], axis=0))
    for c in range(3):
        wide[c, 16 : 16 + rows, TILE:tail] = x[c, :, :]
        wide[c, 16 : 16 + rows, 0:TILE] = pltpu.roll(turned_left, 124 - 4 * c, axis=1)
        wide[c, 16 : 16 + rows, tail:full] = pltpu.roll(turned_right, (TILE - 4 * c) % TILE, axis=1)
        wide[c, 14:16, TILE:tail] = above[4 * c + 2 : 4 * c + 4, 0:columns]
        wide[c, 16 + rows : 18 + rows, TILE:tail] = below[4 * c : 4 * c + 2, 0:columns]
        wide[c, 15:16, 0:TILE] = above[4 * c + 3 : 4 * c + 4, columns : columns + TILE]
        wide[c, 15:16, tail:full] = pltpu.roll(above[4 * c : 4 * c + 1, columns + TILE :], 1, axis=1)
        wide[c, 16 + rows : 17 + rows, 0:TILE] = pltpu.roll(
            below[4 * c + 3 : 4 * c + 4, columns : columns + TILE], TILE - 1, axis=1
        )
        wide[c, 16 + rows : 17 + rows, tail:full] = below[4 * c : 4 * c + 1, columns + TILE :]

    lane = lax.broadcasted_iota(jnp.int32, (8, full), 1)
    sub = lax.broadcasted_iota(jnp.int32, (8, full), 0)
    first_row = jnp.where(flags[0] > 0, 0, -1)
    end_row = jnp.where(flags[1] > 0, rows, rows + 1)
    first_col = jnp.where(flags[2] > 0, 0, -1)
    end_col = jnp.where(flags[3] > 0, columns, columns + 1)
    col = lane - TILE
    in_cols = (col >= first_col) & (col < end_col)

    def bend_tile(t, carry):
        row = sub + (t * 8 - 8)
        inside = in_cols & (row >= first_row) & (row < end_row)
        at = pl.multiple_of(t * 8, 8)
        for c in range(3):
            block = wide[c, pl.ds(at, 24), :]
            center = block[8:16]
            value = (
                (block[9:17] + block[7:15])
                + (pltpu.roll(center, full - 1, axis=1) + pltpu.roll(center, 1, axis=1))
                - 4.0 * center
            )
            curve[c, pl.ds(at, 8), :] = jnp.where(inside, value, 0.0)
        return carry

    lax.fori_loop(0, rows // 8 + 2, bend_tile, 0)

    def force_tile(t, carry):
        at = pl.multiple_of(t * 8, 8)
        beside = []
        centers = []
        bends = []
        for c in range(3):
            block = wide[c, pl.ds(at + 8, 24), :]
            mid = block[8:16]
            beside.append(
                (
                    block[9:17, TILE:tail],
                    block[7:15, TILE:tail],
                    pltpu.roll(mid, full - 1, axis=1)[:, TILE:tail],
                    pltpu.roll(mid, 1, axis=1)[:, TILE:tail],
                )
            )
            centers.append(mid[:, TILE:tail])
            bent = curve[c, pl.ds(at, 24), :]
            middle = bent[8:16]
            bends.append(
                (
                    (bent[9:17, TILE:tail] + bent[7:15, TILE:tail])
                    + (pltpu.roll(middle, full - 1, axis=1) + pltpu.roll(middle, 1, axis=1))[:, TILE:tail]
                )
                - 4.0 * middle[:, TILE:tail]
            )
        total = [None] * 3
        for way in range(4):
            offset = [beside[c][way] - centers[c] for c in range(3)]
            gain = 1.0 + hardening * (offset[0] * offset[0] + offset[1] * offset[1] + offset[2] * offset[2])
            for c in range(3):
                part = offset[c] * gain
                total[c] = part if way == 0 else total[c] + part
        stiff = stiffness[pl.ds(at, 8), :]
        for c in range(3):
            speed = velocity[c, pl.ds(at, 8), :]
            force = stiff * total[c] - bend_gain * bends[c]
            result = speed + time_step * (force - damping * speed)
            for b in range(columns // TILE):
                base[c, pl.ds(at + b * rows, 8), :] = result[:, b * TILE : (b + 1) * TILE]
        return carry

    lax.fori_loop(0, rows // 8, force_tile, 0)


def stencil(flags, x, velocity, stiffness, left, right, above, below):
    _, rows, columns = x.shape
    return pl.pallas_call(
        stencil_kernel,
        out_shape=jax.ShapeDtypeStruct(blocked(x.shape), F32),
        in_specs=[SMEM] + [VMEM] * 7,
        out_specs=VMEM,
        scratch_shapes=[
            pltpu.VMEM((3, rows + 32, columns + 2 * TILE), F32),
            pltpu.VMEM((3, rows + 16, columns + 2 * TILE), F32),
        ],
        name="stencil",
        cost_estimate=pl.CostEstimate(flops=20_000_000, bytes_accessed=6_000_000, transcendentals=0),
    )(flags, x, velocity, stiffness, left, right, above, below)


def split_three(value):
    one = value.astype(BF).astype(F32)
    rest = value - one
    two = rest.astype(BF).astype(F32)
    return one, two, rest - two


def slot_features(received, row):
    sub = lax.broadcasted_iota(jnp.int32, (8, TILE), 0)
    third = sub & 3
    x, y, z = [jnp.broadcast_to(received[pl.ds(row + c, 1), :], (8, TILE)) * SCALE for c in range(3)]
    norm = -0.5 * (x * x + y * y + z * z) + NORM_SHIFT
    place = jnp.where(third == 0, x, jnp.where(third == 1, y, jnp.where(third == 2, z, 0.0)))
    y1, y2, y3 = split_three(place)
    n1, n2, n3 = split_three(norm)
    low = sub < 4
    a = jnp.where(low, y1, y2) + jnp.where(sub == 3, 1.0, 0.0)
    b = jnp.where(low, y3, y1)
    d = jnp.where(low, jnp.where(third == 0, n1, jnp.where(third == 1, n2, n3)), 1.0)
    d = d * jnp.where(third == 3, 0.0, 1.0)

    def turn(value):
        return pltpu.roll(value, 4, axis=0)

    one = jnp.concatenate([a, b, a, d], axis=0).astype(BF)
    other = jnp.concatenate([a, turn(b), turn(a), turn(d)], axis=0).astype(BF)
    return one, other


def pair_kernel(pairs, received, out, acc, w0, w1, g0, g1):
    count = pairs.shape[1]
    slots = received.shape[0] // 3
    sub = lax.broadcasted_iota(jnp.int32, (8, TILE), 0)
    top = sub < 3
    acc[...] = jnp.zeros_like(acc)
    zero = jnp.zeros((32, TILE), BF)

    def weigh(step, weights, held):
        for u in range(GROUP):
            m = step * GROUP + u
            near, near_other = slot_features(received, jnp.maximum(pairs[0, m], 0) * 3)
            far, far_other = slot_features(received, jnp.maximum(pairs[1, m], 0) * 3)
            left = jnp.concatenate([near, far], axis=0)
            right = jnp.concatenate(
                [jnp.concatenate([far_other, zero], axis=1), jnp.concatenate([zero, near_other], axis=1)], axis=0
            )
            exponent = lax.dot_general(left, right, (((0,), (0,)), ((), ())), preferred_element_type=F32)
            weight = jnp.exp2(exponent)
            coarse = weight.astype(BF)
            fine = (weight - coarse.astype(F32)).astype(BF)
            weights[pl.ds(u * 256, 128), :] = coarse
            weights[pl.ds(u * 256 + 128, 128), :] = fine
            held[pl.ds(u * 32, 16), :] = near[:16]
            held[pl.ds(u * 32 + 16, 16), :] = far[:16]

    def push(step, weights, held):
        results = []
        for u in range(GROUP):
            m = step * GROUP + u
            rows = held[pl.ds(u * 32, 32), :]
            total = jnp.dot(
                jnp.concatenate([rows, rows], axis=1), weights[pl.ds(u * 256, 256), :], preferred_element_type=F32
            )
            to_far = total[0:8, :TILE] + jnp.where(top, total[8:16, :TILE], 0.0)
            to_near = total[16:24, TILE:] + jnp.where(top, total[24:32, TILE:], 0.0)
            results.append((pairs[0, m], to_near, pairs[1, m], to_far))
        for near, to_near, far, to_far in results:
            live = near >= 0
            at_near = pl.multiple_of(jnp.where(live, near, slots) * 8, 8)
            at_far = pl.multiple_of(jnp.where(live, far, slots) * 8, 8)
            acc[pl.ds(at_near, 8), :] += to_near
            acc[pl.ds(at_far, 8), :] += to_far

    steps = count // GROUP
    weigh(0, w0, g0)

    def body(t, carry):
        push(2 * t, w0, g0)
        weigh(2 * t + 1, w1, g1)
        push(2 * t + 1, w1, g1)
        weigh(2 * t + 2, w0, g0)
        return carry

    lax.fori_loop(0, steps // 2 - 1, body, 0)
    weigh(steps - 1, w1, g1)
    push(steps - 2, w0, g0)
    push(steps - 1, w1, g1)

    def finish(g, carry):
        def at(row):
            return acc[pl.ds(g * 64 + row, 8, stride=8), :]

        total = at(3)
        for c in range(3):
            near = received[pl.ds(g * 24 + c, 8, stride=3), :]
            out[pl.ds(g * 24 + c, 8, stride=3), :] = near * total - (at(c) + at(4 + c)) * (1.0 / SCALE)
        return carry

    lax.fori_loop(0, slots // 8, finish, 0, unroll=4)


def pair_forces(pairs, received):
    slots = received.shape[0] // 3
    return pl.pallas_call(
        pair_kernel,
        out_shape=jax.ShapeDtypeStruct(received.shape, F32),
        in_specs=[SMEM, VMEM],
        out_specs=VMEM,
        scratch_shapes=[
            pltpu.VMEM(((slots + 1) * 8, TILE), F32),
            pltpu.VMEM((GROUP * 256, 256), BF),
            pltpu.VMEM((GROUP * 256, 256), BF),
            pltpu.VMEM((GROUP * 32, TILE), BF),
            pltpu.VMEM((GROUP * 32, TILE), BF),
        ],
        name="pair",
        cost_estimate=pl.CostEstimate(flops=2_000_000_000, bytes_accessed=2_000_000, transcendentals=8_000_000),
    )(pairs, received)


def advance_kernel(last, route, returned, base, x, *refs):
    if last:
        speed, place, even, odd = refs
    else:
        speed, place, sent, cols, rows_out, even, odd, held = refs
    _, rows, columns = x.shape
    blocks = columns // TILE
    even[...] = base[...]
    odd[...] = jnp.zeros_like(odd)

    def scatter(step, carry):
        for u in range(4):
            for half, target in enumerate((even, odd)):
                slot = step * 8 + 2 * u + half
                row = tile_row(route, slot, rows, blocks)
                for c in range(3):
                    target[c, pl.ds(row, 1), :] += time_step * returned[pl.ds(slot * 3 + c, 1), :]
        return carry

    lax.fori_loop(0, route.shape[0] // 8, scatter, 0)

    def move(t, carry):
        at = pl.multiple_of(t * 8, 8)
        for c in range(3):
            for b in range(blocks):
                inner = pl.ds(at + b * rows, 8)
                outer = slice(b * TILE, (b + 1) * TILE)
                value = even[c, inner, :] + odd[c, inner, :]
                moved = x[c, pl.ds(at, 8), outer] + time_step * value
                speed[c, pl.ds(at, 8), outer] = value
                place[c, pl.ds(at, 8), outer] = moved
                if not last:
                    held[c, inner, :] = moved
        return carry

    lax.fori_loop(0, rows // 8, move, 0)
    if not last:
        pack_tiles(route, held, sent, rows)
        pack_edges(place, cols, rows_out, rows, columns)


def advance(route, returned, base, x, last):
    shapes = (jax.ShapeDtypeStruct(x.shape, F32), jax.ShapeDtypeStruct(x.shape, F32))
    if not last:
        shapes = shapes + packed_shapes(route, x)
    return pl.pallas_call(
        functools.partial(advance_kernel, last),
        out_shape=shapes,
        in_specs=[SMEM, VMEM, VMEM, VMEM],
        out_specs=(VMEM,) * len(shapes),
        scratch_shapes=[pltpu.VMEM(blocked(x.shape), F32)] * (2 if last else 3),
        name="advance",
        cost_estimate=pl.CostEstimate(flops=2_000_000, bytes_accessed=8_000_000, transcendentals=0),
    )(route, returned, base, x)


def exchange(blocks):
    owners = lax.axis_size("gx") * lax.axis_size("gy")
    shaped = blocks.reshape(owners, 3, SLOTS, TILE)
    moved = lax.all_to_all(shaped, ("gx", "gy"), split_axis=0, concat_axis=0, tiled=True)
    return moved.reshape(blocks.shape)


def shift(values, axis):
    count = lax.axis_size(axis)
    return (
        lax.ppermute(values[0], axis, [(i, i + 1) for i in range(count - 1)]),
        lax.ppermute(values[1], axis, [(i + 1, i) for i in range(count - 1)]),
    )


def local(positions, velocity, stiffness, send_tiles, pair_tiles):
    route = send_tiles.reshape(-1)
    paired = pair_tiles.reshape(2, -1)
    row, col = lax.axis_index("gx"), lax.axis_index("gy")
    flags = jnp.stack(
        [row == 0, row == lax.axis_size("gx") - 1, col == 0, col == lax.axis_size("gy") - 1]
    ).astype(jnp.int32)
    sent, cols, rows = pack(route, positions)
    half = positions.shape[1] - TILE
    for repeat in range(STEPS):
        received = exchange(sent)
        left, right = shift((cols, cols), "gy")
        downward = jnp.concatenate([rows, left[:, half:], right[:, half:]], axis=1)
        upward = jnp.concatenate([rows, left[:, :TILE], right[:, :TILE]], axis=1)
        above, below = shift((downward, upward), "gx")
        base = stencil(flags, positions, velocity, stiffness, left, right, above, below)
        returned = exchange(pair_forces(paired, received))
        last = repeat == STEPS - 1
        velocity, positions, *packed = advance(route, returned, base, positions, last)
        if not last:
            sent, cols, rows = packed
    return (positions, velocity)


def solution(mesh):
    return jax.shard_map(
        local,
        mesh=mesh,
        in_specs=(
            P(None, "gx", "gy"),
            P(None, "gx", "gy"),
            P("gx", "gy"),
            P("gx", "gy", None),
            P("gx", "gy", None, None),
        ),
        out_specs=(P(None, "gx", "gy"), P(None, "gx", "gy")),
        check_vma=False,
    )
```

profile of v0, /device:TPU:1, one launch (start us, length us, event | category | flops | bytes accessed | tf_op | source)
XLA Modules:
  0.0 182.2 jit_solution(14996733009021574185)
XLA Ops:
  0.6 3.9 %pack.1 = (f32[1536,128]{1,0:T(8,128)}, f32[16,256]{1,0:T(8,128)}, f32[16,512]{1,0:T(8,128)}) custom-call(s32[512]{0:T(512)} %bitcast.22, f32[3,256,512]{2,1,0:T(8,128)} %x.5), custom_call_target="tpu_custom_call" | custom-call | flops 400000 | bytes 3000000 | tf_op jit(solution)/shard_map/pack/pallas_call | solution.py:94
  4.5 28.4 %all_to_all.20 = f32[128,3,4,128]{3,2,1,0:T(4,128)} all-to-all(f32[128,3,4,128]{3,2,1,0:T(4,128)} %bitcast.19), channel_id=1, replica_groups=mesh['gx'=8,'gy'=16] {'gx','gy'}, dimensions={0} | all-to-all | bytes 1572864 | tf_op jit(solution)/shard_map/all_to_all | solution.py:390
  32.9 18.1 %pair.2 = f32[1536,128]{1,0:T(8,128)} custom-call(s32[2,256]{1,0:T(2,128)} %bitcast.25, f32[1536,128]{1,0:T(8,128)} %bitcast.20), custom_call_target="tpu_custom_call" | custom-call | flops 2000000000 | bytes 2000000 | tf_op jit(solution)/shard_map/pair/pallas_call | solution.py:314
  51.0 4.0 %all-to-all-start.1 = ((f32[128,3,4,128]{3,2,1,0:T(4,128)}), f32[128,3,4,128]{3,2,1,0:T(4,128)S(1)}, u32[]{:S(2)}, u32[]{:S(2)}) async-start(f32[128,3,4,128]{3,2,1,0:T(4,128)} %bitcast.16), calls=%async_computation.1 | async-start | bytes 1572864 | tf_op jit(solution)/shard_map/all_to_all | solution.py:390
  55.0 1.3 collective-permute-start.1
  56.3 4.0 %collective-permute-start = (f32[16,256]{1,0:T(8,128)S(1)}, f32[16,256]{1,0:T(8,128)S(1)}, u32[]{:S(2)}, u32[]{:S(2)}) collective-permute-start(f32[16,256]{1,0:T(8,128)S(1)} %copy-done.12), channel_id=1, source_target_pairs={{0,1},{1,2},{2,3},{3,4},{4,5},{5,6},{6,7},{7,8},{8,9},{9,10},{10,1... | collective-permute-start | bytes 49160 | tf_op jit(solution)/shard_map/ppermute | solution.py:397
  60.3 4.8 %collective-permute-done.1.right = f32[16,256]{1,0:T(8,128)S(1)} collective-permute-done((f32[16,256]{1,0:T(8,128)S(1)}, f32[16,256]{1,0:T(8,128)S(1)}, u32[]{:S(2)}, u32[]{:S(2)}) %collective-permute-start.1) | collective-permute-done | bytes 16416 | tf_op jit(solution)/shard_map/ppermute | solution.py:398
  65.2 2.9 %collective-permute-start.3 = (f32[16,768]{1,0:T(8,128)S(1)}, f32[16,768]{1,0:T(8,128)S(1)}, u32[]{:S(2)}, u32[]{:S(2)}) collective-permute-start(f32[16,768]{1,0:T(8,128)S(1)} %get-tuple-element.24), channel_id=1, source_target_pairs={{16,0},{32,16},{48,32},{64,48},{80,64},{96,80},{112,96},{17,1},{33... | collective-permute-start | bytes 147464 | tf_op jit(solution)/shard_map/ppermute | solution.py:398
  68.1 3.1 %collective-permute-start.2 = (f32[16,768]{1,0:T(8,128)S(1)}, f32[16,768]{1,0:T(8,128)S(1)}, u32[]{:S(2)}, u32[]{:S(2)}) collective-permute-start(f32[16,768]{1,0:T(8,128)S(1)} %get-tuple-element.25), channel_id=1, source_target_pairs={{0,16},{16,32},{32,48},{48,64},{64,80},{80,96},{96,112},{1,17},{17... | collective-permute-start | bytes 147464 | tf_op jit(solution)/shard_map/ppermute | solution.py:397
  73.0 12.7 %stencil.2.base = f32[3,1024,128]{2,1,0:T(8,128)} custom-call(s32[4]{0:T(128)} %add_convert_fusion.flags, f32[3,256,512]{2,1,0:T(8,128)} %x.5, f32[3,256,512]{2,1,0:T(8,128)} %velocity.1, f32[256,512]{1,0:T(8,128)} %stiffness.3, f32[16,256]{1,0:T(8,128)} %copy-done.3, f32[16,256]{1,0:T(8,128)} %copy-done.2, f32[16,768]{1,0:T(8,128)} %copy-done.8, ...), custom_call_target="tpu_custom_call" | custom-call | flops 20000000 | bytes 6000000 | tf_op jit(solution)/shard_map/stencil/pallas_call | solution.py:197
  85.7 0.9 copy-done
  86.6 8.3 %advance.2 = (f32[3,256,512]{2,1,0:T(8,128)}, f32[3,256,512]{2,1,0:T(8,128)}, f32[1536,128]{1,0:T(8,128)}, f32[16,256]{1,0:T(8,128)}, f32[16,512]{1,0:T(8,128)}) custom-call(s32[512]{0:T(512)} %bitcast.23, f32[1536,128]{1,0:T(8,128)} %bitcast.14, f32[3,1024,128]{2,1,0:T(8,128)} %stencil.2.base, f32[3,256,512]{2,1,0:T(8,128)} %x.5), custom_call_target="tpu_custom_call" | custom-call | flops 2000000 | bytes 8000000 | tf_op jit(solution)/shard_map/advance/pallas_call | solution.py:376
  94.9 27.1 %all_to_all.21 = f32[128,3,4,128]{3,2,1,0:T(4,128)} all-to-all(f32[128,3,4,128]{3,2,1,0:T(4,128)} %bitcast.18), channel_id=1, replica_groups=mesh['gx'=8,'gy'=16] {'gx','gy'}, dimensions={0} | all-to-all | bytes 1572864 | tf_op jit(solution)/shard_map/all_to_all | solution.py:390
  121.9 18.1 %pair.3 = f32[1536,128]{1,0:T(8,128)} custom-call(s32[2,256]{1,0:T(2,128)} %bitcast.26, f32[1536,128]{1,0:T(8,128)} %bitcast.21), custom_call_target="tpu_custom_call" | custom-call | flops 2000000000 | bytes 2000000 | tf_op jit(solution)/shard_map/pair/pallas_call | solution.py:314
  140.0 4.0 %all-to-all-start.3 = ((f32[128,3,4,128]{3,2,1,0:T(4,128)}), f32[128,3,4,128]{3,2,1,0:T(4,128)S(1)}, u32[]{:S(2)}, u32[]{:S(2)}) async-start(f32[128,3,4,128]{3,2,1,0:T(4,128)} %bitcast.17), calls=%async_computation.3 | async-start | bytes 1572864 | tf_op jit(solution)/shard_map/all_to_all | solution.py:390
  144.1 1.3 collective-permute-start.5
  145.4 4.0 %collective-permute-start.4 = (f32[16,256]{1,0:T(8,128)S(1)}, f32[16,256]{1,0:T(8,128)S(1)}, u32[]{:S(2)}, u32[]{:S(2)}) collective-permute-start(f32[16,256]{1,0:T(8,128)S(1)} %copy-done.13), channel_id=1, source_target_pairs={{0,1},{1,2},{2,3},{3,4},{4,5},{5,6},{6,7},{7,8},{8,9},{9,10},{10,1... | collective-permute-start | bytes 49160 | tf_op jit(solution)/shard_map/ppermute | solution.py:397
  149.4 4.8 %collective-permute-done.5.right = f32[16,256]{1,0:T(8,128)S(1)} collective-permute-done((f32[16,256]{1,0:T(8,128)S(1)}, f32[16,256]{1,0:T(8,128)S(1)}, u32[]{:S(2)}, u32[]{:S(2)}) %collective-permute-start.5) | collective-permute-done | bytes 16416 | tf_op jit(solution)/shard_map/ppermute | solution.py:398
  154.3 2.9 %collective-permute-start.7 = (f32[16,768]{1,0:T(8,128)S(1)}, f32[16,768]{1,0:T(8,128)S(1)}, u32[]{:S(2)}, u32[]{:S(2)}) collective-permute-start(f32[16,768]{1,0:T(8,128)S(1)} %get-tuple-element.22), channel_id=1, source_target_pairs={{16,0},{32,16},{48,32},{64,48},{80,64},{96,80},{112,96},{17,1},{33... | collective-permute-start | bytes 147464 | tf_op jit(solution)/shard_map/ppermute | solution.py:398
  157.2 3.1 %collective-permute-start.6 = (f32[16,768]{1,0:T(8,128)S(1)}, f32[16,768]{1,0:T(8,128)S(1)}, u32[]{:S(2)}, u32[]{:S(2)}) collective-permute-start(f32[16,768]{1,0:T(8,128)S(1)} %get-tuple-element.23), channel_id=1, source_target_pairs={{0,16},{16,32},{32,48},{48,64},{64,80},{80,96},{96,112},{1,17},{17... | collective-permute-start | bytes 147464 | tf_op jit(solution)/shard_map/ppermute | solution.py:397
  160.4 1.0 collective-permute-done.6.above
  162.0 12.7 %stencil.3.base = f32[3,1024,128]{2,1,0:T(8,128)} custom-call(s32[4]{0:T(128)} %add_convert_fusion.flags, f32[3,256,512]{2,1,0:T(8,128)} %get-tuple-element.16.x, f32[3,256,512]{2,1,0:T(8,128)} %get-tuple-element.17.velocity, f32[256,512]{1,0:T(8,128)} %stiffness.3, f32[16,256]{1,0:T(8,128)} %copy-done.5, f32[16,256]{1,0:T(8,128)} %copy-done.4, ...), custom_call_target="tpu_custom_call" | custom-call | flops 20000000 | bytes 6000000 | tf_op jit(solution)/shard_map/stencil/pallas_call | solution.py:197
  174.7 0.9 copy-done.1
  175.6 6.6 %advance.3 = (f32[3,256,512]{2,1,0:T(8,128)}, f32[3,256,512]{2,1,0:T(8,128)}) custom-call(s32[512]{0:T(512)} %bitcast.24, f32[1536,128]{1,0:T(8,128)} %bitcast.15, f32[3,1024,128]{2,1,0:T(8,128)} %stencil.3.base, f32[3,256,512]{2,1,0:T(8,128)} %get-tuple-element.16.x), custom_call_target="tpu_custom_call" | custom-call | flops 2000000 | bytes 8000000 | tf_op jit(solution)/shard_map/advance/pallas_call | solution.py:376
  (40 shorter events, 2.6 us)
Async XLA Ops:
  51.0 4.0 %copy-start.12 = (f32[16,256]{1,0:T(8,128)S(1)}, f32[16,256]{1,0:T(8,128)}, u32[]{:S(2)}) copy-start(f32[16,256]{1,0:T(8,128)} %get-tuple-element.13) | copy-start | bytes 49156
  51.0 14.2 %copy-start.10 = (f32[16,512]{1,0:T(8,128)S(1)}, f32[16,512]{1,0:T(8,128)}, u32[]{:S(2)}) copy-start(f32[16,512]{1,0:T(8,128)} %get-tuple-element.14) | copy-start | bytes 98308
  51.0 34.7 %all-to-all-start.1 = ((f32[128,3,4,128]{3,2,1,0:T(4,128)}), f32[128,3,4,128]{3,2,1,0:T(4,128)S(1)}, u32[]{:S(2)}, u32[]{:S(2)}) async-start(f32[128,3,4,128]{3,2,1,0:T(4,128)} %bitcast.16), calls=%async_computation.1 | async-start | bytes 1572864 | tf_op jit(solution)/shard_map/all_to_all | solution.py:390
  55.0 10.1 %collective-permute-start.1 = (f32[16,256]{1,0:T(8,128)S(1)}, f32[16,256]{1,0:T(8,128)S(1)}, u32[]{:S(2)}, u32[]{:S(2)}) collective-permute-start(f32[16,256]{1,0:T(8,128)S(1)} %copy-done.12), channel_id=1, source_target_pairs={{1,0},{2,1},{3,2},{4,3},{5,4},{6,5},{7,6},{8,7},{9,8},{10,9},{11,1... | collective-permute-start | bytes 49160 | tf_op jit(solution)/shard_map/ppermute | solution.py:398
  56.3 8.8 %collective-permute-start = (f32[16,256]{1,0:T(8,128)S(1)}, f32[16,256]{1,0:T(8,128)S(1)}, u32[]{:S(2)}, u32[]{:S(2)}) collective-permute-start(f32[16,256]{1,0:T(8,128)S(1)} %copy-done.12), channel_id=1, source_target_pairs={{0,1},{1,2},{2,3},{3,4},{4,5},{5,6},{6,7},{7,8},{8,9},{9,10},{10,1... | collective-permute-start | bytes 49160 | tf_op jit(solution)/shard_map/ppermute | solution.py:397
  65.2 7.2 %copy-start.2 = (f32[16,256]{1,0:T(8,128)}, f32[16,256]{1,0:T(8,128)S(1)}, u32[]{:S(2)}) copy-start(f32[16,256]{1,0:T(8,128)S(1)} %collective-permute-done.1.right) | copy-start | bytes 49156
  65.2 7.2 %copy-start.3 = (f32[16,256]{1,0:T(8,128)}, f32[16,256]{1,0:T(8,128)S(1)}, u32[]{:S(2)}) copy-start(f32[16,256]{1,0:T(8,128)S(1)} %collective-permute-done.left) | copy-start | bytes 49156
  65.2 6.5 %collective-permute-start.3 = (f32[16,768]{1,0:T(8,128)S(1)}, f32[16,768]{1,0:T(8,128)S(1)}, u32[]{:S(2)}, u32[]{:S(2)}) collective-permute-start(f32[16,768]{1,0:T(8,128)S(1)} %get-tuple-element.24), channel_id=1, source_target_pairs={{16,0},{32,16},{48,32},{64,48},{80,64},{96,80},{112,96},{17,1},{33... | collective-permute-start | bytes 147464 | tf_op jit(solution)/shard_map/ppermute | solution.py:398
  68.1 4.2 %collective-permute-start.2 = (f32[16,768]{1,0:T(8,128)S(1)}, f32[16,768]{1,0:T(8,128)S(1)}, u32[]{:S(2)}, u32[]{:S(2)}) collective-permute-start(f32[16,768]{1,0:T(8,128)S(1)} %get-tuple-element.25), channel_id=1, source_target_pairs={{0,16},{16,32},{32,48},{48,64},{64,80},{80,96},{96,112},{1,17},{17... | collective-permute-start | bytes 147464 | tf_op jit(solution)/shard_map/ppermute | solution.py:397
  71.8 0.6 copy-start.6
  72.4 0.6 copy-start.8
  85.7 0.9 copy-start
  140.0 4.1 %copy-start.13 = (f32[16,256]{1,0:T(8,128)S(1)}, f32[16,256]{1,0:T(8,128)}, u32[]{:S(2)}) copy-start(f32[16,256]{1,0:T(8,128)} %get-tuple-element.18) | copy-start | bytes 49156
  140.0 14.2 %copy-start.11 = (f32[16,512]{1,0:T(8,128)S(1)}, f32[16,512]{1,0:T(8,128)}, u32[]{:S(2)}) copy-start(f32[16,512]{1,0:T(8,128)} %get-tuple-element.19) | copy-start | bytes 98308
  140.0 34.7 %all-to-all-start.3 = ((f32[128,3,4,128]{3,2,1,0:T(4,128)}), f32[128,3,4,128]{3,2,1,0:T(4,128)S(1)}, u32[]{:S(2)}, u32[]{:S(2)}) async-start(f32[128,3,4,128]{3,2,1,0:T(4,128)} %bitcast.17), calls=%async_computation.3 | async-start | bytes 1572864 | tf_op jit(solution)/shard_map/all_to_all | solution.py:390
  144.1 10.1 %collective-permute-start.5 = (f32[16,256]{1,0:T(8,128)S(1)}, f32[16,256]{1,0:T(8,128)S(1)}, u32[]{:S(2)}, u32[]{:S(2)}) collective-permute-start(f32[16,256]{1,0:T(8,128)S(1)} %copy-done.13), channel_id=1, source_target_pairs={{1,0},{2,1},{3,2},{4,3},{5,4},{6,5},{7,6},{8,7},{9,8},{10,9},{11,1... | collective-permute-start | bytes 49160 | tf_op jit(solution)/shard_map/ppermute | solution.py:398
  145.4 8.8 %collective-permute-start.4 = (f32[16,256]{1,0:T(8,128)S(1)}, f32[16,256]{1,0:T(8,128)S(1)}, u32[]{:S(2)}, u32[]{:S(2)}) collective-permute-start(f32[16,256]{1,0:T(8,128)S(1)} %copy-done.13), channel_id=1, source_target_pairs={{0,1},{1,2},{2,3},{3,4},{4,5},{5,6},{6,7},{7,8},{8,9},{9,10},{10,1... | collective-permute-start | bytes 49160 | tf_op jit(solution)/shard_map/ppermute | solution.py:397
  154.2 7.2 %copy-start.4 = (f32[16,256]{1,0:T(8,128)}, f32[16,256]{1,0:T(8,128)S(1)}, u32[]{:S(2)}) copy-start(f32[16,256]{1,0:T(8,128)S(1)} %collective-permute-done.5.right) | copy-start | bytes 49156
  154.2 7.2 %copy-start.5 = (f32[16,256]{1,0:T(8,128)}, f32[16,256]{1,0:T(8,128)S(1)}, u32[]{:S(2)}) copy-start(f32[16,256]{1,0:T(8,128)S(1)} %collective-permute-done.4.left) | copy-start | bytes 49156
  154.3 6.1 %collective-permute-start.7 = (f32[16,768]{1,0:T(8,128)S(1)}, f32[16,768]{1,0:T(8,128)S(1)}, u32[]{:S(2)}, u32[]{:S(2)}) collective-permute-start(f32[16,768]{1,0:T(8,128)S(1)} %get-tuple-element.22), channel_id=1, source_target_pairs={{16,0},{32,16},{48,32},{64,48},{80,64},{96,80},{112,96},{17,1},{33... | collective-permute-start | bytes 147464 | tf_op jit(solution)/shard_map/ppermute | solution.py:398
  157.2 4.2 %collective-permute-start.6 = (f32[16,768]{1,0:T(8,128)S(1)}, f32[16,768]{1,0:T(8,128)S(1)}, u32[]{:S(2)}, u32[]{:S(2)}) collective-permute-start(f32[16,768]{1,0:T(8,128)S(1)} %get-tuple-element.23), channel_id=1, source_target_pairs={{0,16},{16,32},{32,48},{48,64},{64,80},{80,96},{96,112},{1,17},{17... | collective-permute-start | bytes 147464 | tf_op jit(solution)/shard_map/ppermute | solution.py:397
  160.4 1.0 copy-start.7
  161.4 0.6 copy-start.9
  174.7 0.9 copy-start.1
where the time goes:
time: 184 us; the launch traced here: 182 us
  Pallas kernels  80.4 us (44%)
  blocking collectives  55.4 us (30%)
  starting transfers between devices  30.5 us (17%)
  waiting for transfers between devices  11.4 us (6%)
  local copies, waits for them, and re-layouts  3.09 us (2%)
    all_to_all x2, blocking collectives, exchange(): lax.all_to_all(shaped, ('gx', 'gy'), split_axis=0, concat_axis=0, tiled=T...  55.4 us
    pallas_call x2, Pallas kernels, pair_forces(): pl.pallas_call(pair_kernel, out_shape=jax.ShapeDtypeStruct(received.shape...  36.2 us
    pallas_call x2, Pallas kernels, stencil(): pl.pallas_call(stencil_kernel, out_shape=jax.ShapeDtypeStruct(blocked(x.s...  25.3 us
    pallas_call x2, Pallas kernels, advance(): pl.pallas_call(functools.partial(advance_kernel, last), out_shape=shapes,...  14.9 us
    ppermute x4, starting transfers between devices, shift(): lax.ppermute(values[0], axis, [(i, i + 1) for i in range(count - 1)])  14.1 us
    ppermute x4, waiting for transfers between devices, shift(): lax.ppermute(values[1], axis, [(i + 1, i) for i in range(count - 1)])  9.79 us
    ppermute x4, starting transfers between devices, shift(): lax.ppermute(values[1], axis, [(i + 1, i) for i in range(count - 1)])  8.34 us
    all_to_all x2, starting transfers between devices, exchange(): lax.all_to_all(shaped, ('gx', 'gy'), split_axis=0, concat_axis=0, tiled=T...  8.07 us
  transfers between devices with their start and end apart: 10, of which 5 were waited for; matrix products, arithmetic and copies ran while one was open for 0% of the time, Pallas kernels for 14%

commit v1 on v0

v1 whole, which is shorter than its diff:
```python
import functools
import math

import jax
import jax.numpy as jnp
from jax import lax
from jax.experimental import pallas as pl
from jax.experimental.pallas import tpu as pltpu
from jax.sharding import PartitionSpec as P

TILE = 128
STEPS = 2
SLOTS = 4
BLOCK = 3 * SLOTS + 1
GROUP = 16
DEPTH = 2

time_step = 0.1
damping = 0.2
hardening = 0.1
bend_gain = 0.02
contact_gain = 0.25
inverse_width = 0.5

BF = jnp.bfloat16
F32 = jnp.float32

SCALE = math.sqrt(2.0 * inverse_width * math.log2(math.e))
GAIN_LOG = math.log2(contact_gain)
NORM_SHIFT = GAIN_LOG / 2.0

VMEM = pl.BlockSpec(memory_space=pltpu.VMEM)
SMEM = pl.BlockSpec(memory_space=pltpu.SMEM)
ANY = pl.BlockSpec(memory_space=pl.ANY)
HBM = pl.BlockSpec(memory_space=pltpu.HBM)
LIMIT = pltpu.CompilerParams(vmem_limit_bytes=67_043_328)
ROOM = pltpu.CompilerParams(vmem_limit_bytes=40 * 2**20)


def pack_tiles(route, held, sent, corners):
    def body(step, carry):
        for u in range(8):
            slot = step * 8 + u
            row = route[slot]
            to = (step * 2 + u // SLOTS) * BLOCK + (u % SLOTS) * 3
            for c in range(3):
                sent[pl.ds(to + c, 1), :] = held[c, pl.ds(row, 1), :]
        for u in range(2):
            sent[pl.ds((step * 2 + u) * BLOCK + BLOCK - 1, 1), :] = corners
        return carry

    lax.fori_loop(0, route.shape[0] // 8, body, 0)


def pack_edges(held, cols, rows_out, rows):
    blocks = held.shape[1] // rows
    lane = lax.broadcasted_iota(jnp.int32, (rows, TILE), 1)
    mixed = jnp.zeros((rows, TILE), F32)
    for c in range(3):
        head = held[c, 0:rows, :]
        tail = held[c, (blocks - 1) * rows :, :]
        if c:
            head = pltpu.roll(head, 4 * c, axis=1)
        tail = pltpu.roll(tail, 4 * c + 4, axis=1)
        mixed = jnp.where((lane == 4 * c) | (lane == 4 * c + 1), head, mixed)
        mixed = jnp.where((lane == 4 * c + 2) | (lane == 4 * c + 3), tail, mixed)
    cols[...] = jnp.transpose(mixed)[0:16, :]
    for b in range(blocks):
        part = slice(b * TILE, (b + 1) * TILE)
        for c in range(3):
            rows_out[4 * c : 4 * c + 2, part] = held[c, b * rows : b * rows + 2, :]
            rows_out[4 * c + 2 : 4 * c + 4, part] = held[c, (b + 1) * rows - 2 : (b + 1) * rows, :]
        rows_out[12:16, part] = jnp.zeros((4, TILE), F32)
    return jnp.where(lane[0:1] < 16, mixed[0:1], pltpu.roll(mixed[rows - 8 :], 16, axis=1)[7:8])


def block_copies(whole, held, sems, rows, outward=False):
    blocks = whole.shape[2] // TILE
    copies = []
    for c in range(3):
        for b in range(blocks):
            far = whole.at[c, :, pl.ds(b * TILE, TILE)]
            near = held(c, b)
            pair = (near, far) if outward else (far, near)
            copies.append(pltpu.make_async_copy(*pair, sems.at[c * blocks + b]))
    return copies


def pack_kernel(route, x, sent, cols, rows_out, held, sems):
    rows = x.shape[1]
    copies = block_copies(x, lambda c, b: held.at[c, pl.ds(b * rows, rows), :], sems, rows)
    for copy in copies:
        copy.start()
    for copy in copies:
        copy.wait()
    corners = pack_edges(held, cols, rows_out, rows)
    pack_tiles(route, held, sent, corners)


def blocked(shape):
    return (shape[0], shape[1] * shape[2] // TILE, TILE)


def packed_shapes(route, x):
    _, rows, columns = x.shape
    return (
        jax.ShapeDtypeStruct((route.shape[0] // SLOTS * BLOCK, TILE), F32),
        jax.ShapeDtypeStruct((16, rows), F32),
        jax.ShapeDtypeStruct((16, columns), F32),
    )


def pack(route, x):
    return pl.pallas_call(
        pack_kernel,
        out_shape=packed_shapes(route, x),
        in_specs=[SMEM, HBM],
        out_specs=(VMEM, VMEM, VMEM),
        scratch_shapes=[pltpu.VMEM(blocked(x.shape), F32), pltpu.SemaphoreType.DMA((3 * x.shape[2] // TILE,))],
        compiler_params=LIMIT,
        name="pack",
        cost_estimate=pl.CostEstimate(flops=400_000, bytes_accessed=3_000_000, transcendentals=0),
    )(route, x)


def stencil_kernel(
    flags, x, velocity, stiffness, col_a, col_b, row_a, row_b, received, forces, base, wide, curve, edge, speed, stiff, angles, sems, more
):
    _, rows, columns = x.shape
    blocks = columns // TILE
    copies = block_copies(x, lambda c, b: wide.at[c, b + 1, pl.ds(16, rows), :], sems, rows)
    ends = []
    for k in range(4):
        row = jnp.maximum(flags[6 + k], 0) * BLOCK + BLOCK - 1
        tile = pl.ds(pl.multiple_of(row - lax.rem(row, 8), 8), 8)
        ends.append(pltpu.make_async_copy(received.at[tile, :], angles.at[k], more.at[2 + k]))
        ends[-1].start()
    copies.append(pltpu.make_async_copy(velocity, speed, more.at[0]))
    copies.append(pltpu.make_async_copy(stiffness, stiff, more.at[1]))
    for copy in copies:
        copy.start()

    odd_col, odd_row = flags[4] > 0, flags[5] > 0
    left = jnp.where(odd_col, col_a[...], col_b[...])
    right = jnp.where(odd_col, col_b[...], col_a[...])
    fill = jnp.zeros((TILE - 16, rows), F32)
    turned_left = jnp.transpose(jnp.concatenate([left, fill], axis=0))
    turned_right = jnp.transpose(jnp.concatenate([right, fill], axis=0))

    for c in range(3):
        wide[c, 0, 16 : 16 + rows, :] = pltpu.roll(turned_left, 124 - 4 * c, axis=1)
        wide[c, blocks + 1, 16 : 16 + rows, :] = pltpu.roll(turned_right, (TILE - 4 * c) % TILE, axis=1)
    for b in range(blocks):
        part = slice(b * TILE, (b + 1) * TILE)
        above = jnp.where(odd_row, row_a[:, part], row_b[:, part])
        below = jnp.where(odd_row, row_b[:, part], row_a[:, part])
        for c in range(3):
            wide[c, b + 1, 14:16, :] = above[4 * c + 2 : 4 * c + 4]
            wide[c, b + 1, 16 + rows : 18 + rows, :] = below[4 * c : 4 * c + 2]
    for copy in ends:
        copy.wait()
    sub = lax.broadcasted_iota(jnp.int32, (8, TILE), 0)
    for k, (block, row, to, lane_of) in enumerate(
        ((0, 15, TILE - 1, 19), (blocks + 1, 15, 0, 16), (0, 16 + rows, TILE - 1, 3), (blocks + 1, 16 + rows, 0, 0))
    ):
        want = lax.rem(jnp.maximum(flags[6 + k], 0) * BLOCK + BLOCK - 1, 8)
        angle = jnp.where((sub == want) & (flags[6 + k] >= 0), angles[k], 0.0)
        angle = jnp.sum(angle, axis=0, keepdims=True)
        for c in range(3):
            wide[c, block, row : row + 1, :] = pltpu.roll(angle, (to - lane_of - 4 * c) % TILE, axis=1)
    for copy in copies[:-2]:
        copy.wait()

    lane = lax.broadcasted_iota(jnp.int32, (8, TILE), 1)
    at_first, at_last = lane == 0, lane == TILE - 1

    def from_left(turned, b):
        return jnp.where(at_first, turned[b - 1], turned[b])

    def from_right(turned, b):
        return jnp.where(at_last, turned[b + 1], turned[b])

    keep_left = jnp.where(flags[2] > 0, 0.0, 1.0)
    keep_right = jnp.where(flags[3] > 0, 0.0, 1.0)

    def bend_tile(t, carry):
        at = pl.multiple_of(t * 8, 8)
        for c in range(3):
            center = [wide[c, b, pl.ds(at + 8, 8), :] for b in range(blocks + 2)]
            up_turn = [pltpu.roll(v, 1, axis=1) for v in center]
            down_turn = [pltpu.roll(v, TILE - 1, axis=1) for v in center]
            for b in range(blocks + 2):
                value = wide[c, b, pl.ds(at + 9, 8), :] + wide[c, b, pl.ds(at + 7, 8), :]
                right_side = from_right(down_turn, b) if b <= blocks else down_turn[b]
                left_side = from_left(up_turn, b) if b else up_turn[b]
                value = (value + (right_side + left_side)) - 4.0 * center[b]
                if b == 0:
                    value = value * keep_left
                if b == blocks + 1:
                    value = value * keep_right
                curve[c, b, pl.ds(at, 8), :] = value
        return carry

    lax.fori_loop(0, rows // 8 + 2, bend_tile, 0, unroll=2)
    keep_above = jnp.where(flags[0] > 0, 0.0, 1.0)
    keep_below = jnp.where(flags[1] > 0, 0.0, 1.0)
    for c in range(3):
        for b in range(1, blocks + 1):
            curve[c, b, 7:8, :] = curve[c, b, 7:8, :] * keep_above
            curve[c, b, 8 + rows : 9 + rows, :] = curve[c, b, 8 + rows : 9 + rows, :] * keep_below
    for copy in copies[-2:]:
        copy.wait()

    def spring(offset):
        gain = 1.0 + hardening * (offset[0] * offset[0] + offset[1] * offset[1] + offset[2] * offset[2])
        return [v * gain for v in offset]

    def vertical(at, b):
        force = spring([wide[c, b, pl.ds(at + 17, 8), :] - wide[c, b, pl.ds(at + 16, 8), :] for c in range(3)])
        for c in range(3):
            edge[c, b - 1, pl.ds(at + 8, 8), :] = force[c]
        return force

    for b in range(1, blocks + 1):
        vertical(-8, b)

    def force_tile(t, carry):
        at = pl.multiple_of(t * 8, 8)
        center = [[wide[c, b, pl.ds(at + 16, 8), :] for b in range(blocks + 2)] for c in range(3)]
        turned = [[pltpu.roll(v, TILE - 1, axis=1) for v in center[c]] for c in range(3)]
        flat = [spring([from_right(turned[c], b) - center[c][b] for c in range(3)]) for b in range(blocks + 1)]
        for b in range(1, blocks + 1):
            down = vertical(at, b)
            for c in range(3):
                before = jnp.where(
                    at_first, pltpu.roll(flat[b - 1][c], 1, axis=1), pltpu.roll(flat[b][c], 1, axis=1)
                )
                pull = (down[c] - edge[c, b - 1, pl.ds(at + 7, 8), :]) + (flat[b][c] - before)
                middle = curve[c, b, pl.ds(at + 8, 8), :]
                beside = [curve[c, b + k, pl.ds(at + 8, 8), :] for k in (-1, 1)]
                left_side = jnp.where(at_first, pltpu.roll(beside[0], 1, axis=1), pltpu.roll(middle, 1, axis=1))
                right_side = jnp.where(
                    at_last, pltpu.roll(beside[1], TILE - 1, axis=1), pltpu.roll(middle, TILE - 1, axis=1)
                )
                bent = (
                    (curve[c, b, pl.ds(at + 9, 8), :] + curve[c, b, pl.ds(at + 7, 8), :]) + (right_side + left_side)
                ) - 4.0 * middle
                part = slice((b - 1) * TILE, b * TILE)
                was = speed[c, pl.ds(at, 8), part]
                force = stiff[pl.ds(at, 8), part] * pull - bend_gain * bent
                base[c, pl.ds(at + (b - 1) * rows, 8), :] = was + time_step * (force - damping * was)
        return carry

    lax.fori_loop(0, rows // 8, force_tile, 0, unroll=2)


def stencil(flags, x, velocity, stiffness, col_a, col_b, row_a, row_b, received, forces):
    _, rows, columns = x.shape
    blocks = columns // TILE
    return pl.pallas_call(
        stencil_kernel,
        out_shape=jax.ShapeDtypeStruct(blocked(x.shape), F32),
        in_specs=[SMEM, HBM, HBM, HBM] + [VMEM] * 4 + [ANY, ANY],
        out_specs=VMEM,
        scratch_shapes=[
            pltpu.VMEM((3, blocks + 2, rows + 32, TILE), F32),
            pltpu.VMEM((3, blocks + 2, rows + 16, TILE), F32),
            pltpu.VMEM((3, blocks, rows + 8, TILE), F32),
            pltpu.VMEM(x.shape, F32),
            pltpu.VMEM((rows, columns), F32),
            pltpu.VMEM((4, 8, TILE), F32),
            pltpu.SemaphoreType.DMA((3 * blocks,)),
            pltpu.SemaphoreType.DMA((6,)),
        ],
        compiler_params=LIMIT,
        name="stencil",
        cost_estimate=pl.CostEstimate(flops=20_000_000, bytes_accessed=6_000_000, transcendentals=0),
    )(flags, x, velocity, stiffness, col_a, col_b, row_a, row_b, received, forces)


def split_three(value):
    one = value.astype(BF).astype(F32)
    rest = value - one
    two = rest.astype(BF).astype(F32)
    return one, two, rest - two


def pair_kernel(pairs, received, col_a, col_b, row_a, row_b, out, acc, q1, q2, q3, w0, w1, g0, g1):
    count = pairs.shape[1]
    owners = received.shape[0] // BLOCK
    slots = owners * SLOTS
    sub = lax.broadcasted_iota(jnp.int32, (8, TILE), 0)
    low = sub < 4
    spare = (sub & 3) == 3
    sub16 = lax.broadcasted_iota(jnp.int32, (16, TILE), 0)
    upper = ((sub16 & 7) < 4).astype(BF)
    lower = ((sub16 & 7) >= 4).astype(BF)
    acc[...] = jnp.zeros_like(acc)

    def prepare(g, carry):
        for k in range(SLOTS):
            place = [received[pl.ds(g * 8 * BLOCK + 3 * k + c, 8, stride=BLOCK), :] * SCALE for c in range(3)]
            norm = -0.5 * (place[0] * place[0] + place[1] * place[1] + place[2] * place[2]) + NORM_SHIFT
            at = (k * owners + g * 8) * 8
            for r, value in enumerate((*place, norm)):
                for q, part in zip((q1, q2, q3), split_three(value)):
                    q[pl.ds(at + r, 8, stride=8), :] = part
                    q[pl.ds(at + r + 4, 8, stride=8), :] = part
        return carry

    lax.fori_loop(0, owners // 8, prepare, 0)

    def tile_at(slot):
        return pl.multiple_of((lax.rem(slot, SLOTS) * owners + lax.div(slot, SLOTS)) * 8, 8)

    def weigh_one(step, u, weights, held):
        m = step * GROUP + u
        near = pl.ds(tile_at(jnp.maximum(pairs[0, m], 0)), 8)
        far = pl.ds(tile_at(jnp.maximum(pairs[1, m], 0)), 8)
        v, s = [], []
        for q in (q1, q2, q3):
            a, b = q[near, :], q[far, :]
            v.append(jnp.where(low, a, b))
            s.append(jnp.where(low, b, a))
        ones = jnp.where(spare, 1.0, v[0])
        s_ones = jnp.where(spare, 1.0, s[0])
        first = jnp.concatenate([ones, v[1]], axis=0).astype(BF)
        second = jnp.concatenate([jnp.where(spare, v[0], v[1]), v[2]], axis=0).astype(BF)
        third = jnp.concatenate([ones, ones], axis=0).astype(BF)
        left = jnp.concatenate([first, second, third], axis=0)
        right = [
            jnp.concatenate([s[0], s_ones], axis=0).astype(BF),
            jnp.concatenate([jnp.where(spare, 1.0, s[1]), s_ones], axis=0).astype(BF),
            jnp.concatenate([s[1], s[2]], axis=0).astype(BF),
        ]
        right = jnp.concatenate(
            [jnp.concatenate([r * upper for r in right], axis=0), jnp.concatenate([r * lower for r in right], axis=0)], axis=1
        )
        held[pl.ds(u * 32, 16), :] = first
        held[pl.ds(u * 32 + 16, 16), :] = second
        return lax.dot_general(left, right, (((0,), (0,)), ((), ())), preferred_element_type=F32)

    def split_one(exponent, u, weights):
        weight = jnp.exp2(exponent)
        coarse = weight.astype(BF)
        fine = (weight - coarse.astype(F32)).astype(BF)
        weights[pl.ds(u * 256, 128), :] = coarse
        weights[pl.ds(u * 256 + 128, 128), :] = fine

    def push_one(step, u, weights, held):
        m = step * GROUP + u
        rows = held[pl.ds(u * 32, 32), :]
        total = jnp.dot(
            jnp.concatenate([rows, rows], axis=1), weights[pl.ds(u * 256, 256), :], preferred_element_type=F32
        )
        rest = jnp.where(spare, 0.0, total[8:16, :TILE] + total[24:32, :TILE])
        to_far = total[0:8, :TILE] + rest
        rest = jnp.where(spare, 0.0, total[8:16, TILE:] + total[24:32, TILE:])
        to_near = pltpu.roll(total[0:8, TILE:] + rest, 4, axis=0)
        return (pairs[0, m], to_near, pairs[1, m], to_far)

    def add_all(results):
        for near, to_near, far, to_far in results:
            live = near >= 0
            at_near = pl.multiple_of(jnp.where(live, tile_at(near), slots * 8), 8)
            at_far = pl.multiple_of(jnp.where(live, tile_at(far), slots * 8), 8)
            acc[pl.ds(at_near, 8), :] += to_near
            acc[pl.ds(at_far, 8), :] += to_far

    def weigh(step, weights, held):
        for u in range(GROUP):
            split_one(weigh_one(step, u, weights, held), u, weights)

    def push(step, weights, held):
        add_all([push_one(step, u, weights, held) for u in range(GROUP)])

    def both(step, wa, ga, wb, gb):
        results = []
        for u in range(GROUP):
            if u == 0:
                queue = [weigh_one(step + 1, k, wb, gb) for k in range(DEPTH)]
            if u + DEPTH < GROUP:
                queue.append(weigh_one(step + 1, u + DEPTH, wb, gb))
            results.append(push_one(step, u, wa, ga))
            split_one(queue.pop(0), u, wb)
        add_all(results)

    steps = count // GROUP
    weigh(0, w0, g0)

    def body(t, carry):
        both(2 * t, w0, g0, w1, g1)
        both(2 * t + 1, w1, g1, w0, g0)
        return carry

    lax.fori_loop(0, steps // 2 - 1, body, 0)
    both(steps - 2, w0, g0, w1, g1)
    push(steps - 1, w1, g1)

    def finish(g, carry):
        for k in range(SLOTS):

            def at(row):
                return acc[pl.ds((k * owners + g * 8) * 8 + row, 8, stride=8), :]

            total = at(3)
            for c in range(3):
                near = received[pl.ds(g * 8 * BLOCK + 3 * k + c, 8, stride=BLOCK), :]
                to = pl.ds((g * 8 * SLOTS + k) * 3 + c, 8, stride=3 * SLOTS)
                out[to, :] = near * total - at(c) * (1.0 / SCALE)
        return carry

    lax.fori_loop(0, owners // 8, finish, 0)


def pair_forces(pairs, received, col_a, col_b, row_a, row_b):
    slots = received.shape[0] // BLOCK * SLOTS
    return pl.pallas_call(
        pair_kernel,
        out_shape=jax.ShapeDtypeStruct((slots * 3, TILE), F32),
        in_specs=[SMEM, VMEM, ANY, ANY, ANY, ANY],
        out_specs=VMEM,
        compiler_params=ROOM,
        scratch_shapes=[
            pltpu.VMEM(((slots + 1) * 8, TILE), F32),
            pltpu.VMEM((slots * 8, TILE), F32),
            pltpu.VMEM((slots * 8, TILE), F32),
            pltpu.VMEM((slots * 8, TILE), F32),
            pltpu.VMEM((GROUP * 256, 256), BF),
            pltpu.VMEM((GROUP * 256, 256), BF),
            pltpu.VMEM((GROUP * 32, TILE), BF),
            pltpu.VMEM((GROUP * 32, TILE), BF),
        ],
        name="pair",
        cost_estimate=pl.CostEstimate(flops=2_000_000_000, bytes_accessed=2_000_000, transcendentals=8_000_000),
    )(pairs, received, col_a, col_b, row_a, row_b)


def advance_kernel(last, route, returned, base, x, *refs):
    if last:
        speed, place, even, odd, held, start, incoming, sems, more, outs = refs
    else:
        speed, place, sent, cols, rows_out, even, odd, held, start, incoming, sems, more, outs = refs
    _, rows, columns = x.shape
    blocks = columns // TILE

    def block(ref):
        return lambda c, b: ref.at[c, pl.ds(b * rows, rows), :]

    arrive = pltpu.make_async_copy(returned, incoming, more.at[0])
    begin = pltpu.make_async_copy(base, start, more.at[1])
    places = block_copies(x, block(held), sems, rows)
    for copy in (arrive, begin, *places):
        copy.start()
    even[...] = jnp.zeros_like(even)
    odd[...] = jnp.zeros_like(odd)
    arrive.wait()

    def scatter(step, carry):
        for u in range(4):
            for half, target in enumerate((even, odd)):
                slot = step * 8 + 2 * u + half
                row = route[slot]
                for c in range(3):
                    target[c, pl.ds(row, 1), :] += incoming[pl.ds(slot * 3 + c, 1), :]
        return carry

    lax.fori_loop(0, route.shape[0] // 8, scatter, 0)
    begin.wait()
    for copy in places:
        copy.wait()
    leave = block_copies(speed, block(even), outs.at[0], rows, True)
    leave += block_copies(place, block(held), outs.at[1], rows, True)
    half = len(leave) // 2
    for c in range(3):
        for b in range(blocks):

            def move(t, carry):
                inner = pl.ds(pl.multiple_of(t * 8, 8) + b * rows, 8)
                value = start[c, inner, :] + time_step * (even[c, inner, :] + odd[c, inner, :])
                even[c, inner, :] = value
                held[c, inner, :] = held[c, inner, :] + time_step * value
                return carry

            lax.fori_loop(0, rows // 8, move, 0, unroll=8)
            leave[c * blocks + b].start()
            leave[half + c * blocks + b].start()
    if not last:
        corners = pack_edges(held, cols, rows_out, rows)
        pack_tiles(route, held, sent, corners)
    for copy in leave:
        copy.wait()


def advance(route, returned, base, x, last):
    count = 3 * x.shape[2] // TILE
    shapes = (jax.ShapeDtypeStruct(x.shape, F32), jax.ShapeDtypeStruct(x.shape, F32))
    specs = (HBM, HBM)
    if not last:
        shapes = shapes + packed_shapes(route, x)
        specs = specs + (VMEM, VMEM, VMEM)
    return pl.pallas_call(
        functools.partial(advance_kernel, last),
        out_shape=shapes,
        in_specs=[SMEM, ANY, HBM, HBM],
        out_specs=specs,
        scratch_shapes=[pltpu.VMEM(blocked(x.shape), F32)] * 4
        + [
            pltpu.VMEM(returned.shape, F32),
            pltpu.SemaphoreType.DMA((count,)),
            pltpu.SemaphoreType.DMA((2,)),
            pltpu.SemaphoreType.DMA((2, count)),
        ],
        compiler_params=LIMIT,
        name="advance",
        cost_estimate=pl.CostEstimate(flops=2_000_000, bytes_accessed=8_000_000, transcendentals=0),
    )(route, returned, base, x)


def exchange(blocks):
    owners = lax.axis_size("gx") * lax.axis_size("gy")
    height = blocks.shape[0] // owners
    shaped = blocks.reshape((owners, 3, SLOTS, TILE) if height % SLOTS == 0 else (owners, height, 1, TILE))
    moved = lax.all_to_all(shaped, ("gx", "gy"), split_axis=0, concat_axis=0, tiled=True)
    return moved.reshape(blocks.shape)


def swap(value, axis):
    count = lax.axis_size(axis)
    both = [[(i + k, i + 1 - k) for i in range(first, count - 1, 2) for k in range(2)] for first in range(2)]
    return [lax.ppermute(value, axis, pairs) for pairs in both]


def local(positions, velocity, stiffness, send_tiles, pair_tiles):
    tile = jnp.maximum(send_tiles.reshape(-1), 0)
    blocks = positions.shape[2] // TILE
    route = lax.rem(tile, blocks) * positions.shape[1] + lax.div(tile, blocks)
    paired = pair_tiles.reshape(2, -1)
    row, col = lax.axis_index("gx"), lax.axis_index("gy")
    near = [(row + i, col + j) for i in (-1, 1) for j in (-1, 1)]
    flags = jnp.stack(
        [row == 0, row == lax.axis_size("gx") - 1, col == 0, col == lax.axis_size("gy") - 1, col % 2 == 1, row % 2 == 1]
        + [
            jnp.where((i >= 0) & (i < lax.axis_size("gx")) & (j >= 0) & (j < lax.axis_size("gy")), i * lax.axis_size("gy") + j, -1)
            for i, j in near
        ]
    ).astype(jnp.int32)
    sent, cols, rows = pack(route, positions)
    for repeat in range(STEPS):
        received = exchange(sent)
        col_a, col_b = swap(cols, "gy")
        row_a, row_b = swap(rows, "gx")
        forces = pair_forces(paired, received, col_a, col_b, row_a, row_b)
        returned = exchange(forces)
        base = stencil(flags, positions, velocity, stiffness, col_a, col_b, row_a, row_b, received, forces)
        last = repeat == STEPS - 1
        velocity, positions, *packed = advance(route, returned, base, positions, last)
        if not last:
            sent, cols, rows = packed
    return (positions, velocity)


def solution(mesh):
    return jax.shard_map(
        local,
        mesh=mesh,
        in_specs=(
            P(None, "gx", "gy"),
            P(None, "gx", "gy"),
            P("gx", "gy"),
            P("gx", "gy", None),
            P("gx", "gy", None, None),
        ),
        out_specs=(P(None, "gx", "gy"), P(None, "gx", "gy")),
        check_vma=False,
    )
```

time: 184 us -> 140 us (0.76)
  blocking collectives: 55.4 us -> 0 us
  waiting for transfers between devices: 11.4 us -> 27.7 us
  Pallas kernels: 80.4 us -> 65.9 us
  starting transfers between devices: 30.5 us -> 42.8 us
  local copies, waits for them, and re-layouts: 3.09 us -> 0.68 us
    all_to_all x2 -> x0, blocking collectives: 55.4 us -> none  [exchange(): lax.all_to_all(shaped, ('gx', 'gy'), split_axis=0, concat_axis=0, tiled=T...]
    all_to_all x2 -> x4, waiting for transfers between devices: 0.01 us -> 22 us  [exchange(): lax.all_to_all(shaped, ('gx', 'gy'), split_axis=0, concat_axis=0, tiled=T...]
    all_to_all x2 -> x4, starting transfers between devices: 8.07 us -> 26.8 us  [exchange(): lax.all_to_all(shaped, ('gx', 'gy'), split_axis=0, concat_axis=0, tiled=T...]
    pallas_call x2, Pallas kernels: 36.2 us -> 24.1 us  [pair_forces(): pl.pallas_call(pair_kernel, out_shape=jax.ShapeDtypeStruct((slots * 3, TI...]
    ppermute x8, starting transfers between devices: 22.4 us -> 16 us  [swap(): return [lax.ppermute(value, axis, pairs) for pairs in both]]
    ppermute x8, waiting for transfers between devices: 11.4 us -> 5.62 us  [swap(): return [lax.ppermute(value, axis, pairs) for pairs in both]]
    unnamed x28 -> x32, local copies, waits for them, and re-layouts: 3.08 us -> 0.07 us
  transfers between devices with their start and end apart: 10 -> 12, of which waited for: 5 -> 6; matrix products, arithmetic and copies ran while one was open for 0% -> 0% of each run, Pallas kernels for 14% -> 17%
where the time goes in v1:
time: 140 us; the launch traced here: 139 us
  Pallas kernels  65.9 us (47%)
  starting transfers between devices  42.8 us (31%)
  waiting for transfers between devices  27.7 us (20%)
    all_to_all x4, starting transfers between devices, exchange(): lax.all_to_all(shaped, ('gx', 'gy'), split_axis=0, concat_axis=0, tiled=T...  26.8 us
    pallas_call x2, Pallas kernels, pair_forces(): pl.pallas_call(pair_kernel, out_shape=jax.ShapeDtypeStruct((slots * 3, TI...  24.1 us
    pallas_call x2, Pallas kernels, stencil(): pl.pallas_call(stencil_kernel, out_shape=jax.ShapeDtypeStruct(blocked(x.s...  23.7 us
    all_to_all x4, waiting for transfers between devices, exchange(): lax.all_to_all(shaped, ('gx', 'gy'), split_axis=0, concat_axis=0, tiled=T...  22 us
    ppermute x8, starting transfers between devices, swap(): return [lax.ppermute(value, axis, pairs) for pairs in both]  16 us
    pallas_call x2, Pallas kernels, advance(): pl.pallas_call(functools.partial(advance_kernel, last), out_shape=shapes,...  13.5 us
    ppermute x8, waiting for transfers between devices, swap(): return [lax.ppermute(value, axis, pairs) for pairs in both]  5.62 us
    pallas_call x1, Pallas kernels, pack(): pl.pallas_call(pack_kernel, out_shape=packed_shapes(route, x), in_specs=[...  4.62 us
  transfers between devices with their start and end apart: 12, of which 6 were waited for; matrix products, arithmetic and copies ran while one was open for 0% of the time, Pallas kernels for 17%

profile of v1, /device:TPU:1, one launch (start us, length us, event | category | flops | bytes accessed | tf_op | source)
XLA Modules:
  0.0 139.2 jit_solution(4641156824694528611)
XLA Ops:
  0.6 1.3 shift-right-logical_add_fusion
  1.9 4.6 %pack.1 = (f32[1664,128]{1,0:T(8,128)}, f32[16,256]{1,0:T(8,128)}, f32[16,512]{1,0:T(8,128)}) custom-call(s32[512]{0:T(512)} %bitcast.28, f32[3,256,512]{2,1,0:T(8,128)} %x.5), custom_call_target="tpu_custom_call" | custom-call | flops 400000 | bytes 3000000 | tf_op jit(solution)/shard_map/pack/pallas_call | solution.py:114
  6.6 11.5 %all-to-all-start = ((f32[128,13,1,128]{3,2,1,0:T(1,128)}), f32[128,13,1,128]{3,2,1,0:T(1,128)S(1)}, u32[]{:S(2)}, u32[]{:S(2)}) async-start(f32[128,13,1,128]{3,2,1,0:T(1,128)} %bitcast.27), calls=%async_computation | async-start | bytes 1703936 | tf_op jit(solution)/shard_map/all_to_all | solution.py:524
  18.1 3.5 %collective-permute-start.3 = (f32[16,512]{1,0:T(8,128)S(1)}, f32[16,512]{1,0:T(8,128)S(1)}, u32[]{:S(2)}, u32[]{:S(2)}) collective-permute-start(f32[16,512]{1,0:T(8,128)S(1)} %copy-done.13), channel_id=1, source_target_pairs={{16,32},{32,16},{48,64},{64,48},{80,96},{96,80},{17,33},{33,17},{4... | collective-permute-start | bytes 98312 | tf_op jit(solution)/shard_map/ppermute | solution.py:531
  21.7 0.7 collective-permute-start.1
  22.4 3.7 %collective-permute-start = (f32[16,256]{1,0:T(8,128)S(1)}, f32[16,256]{1,0:T(8,128)S(1)}, u32[]{:S(2)}, u32[]{:S(2)}) collective-permute-start(f32[16,256]{1,0:T(8,128)S(1)} %copy-done.15), channel_id=1, source_target_pairs={{0,1},{1,0},{2,3},{3,2},{4,5},{5,4},{6,7},{7,6},{8,9},{9,8},{10,11... | collective-permute-start | bytes 49160 | tf_op jit(solution)/shard_map/ppermute | solution.py:531
  26.1 2.8 %collective-permute-done.col_a = f32[16,256]{1,0:T(8,128)S(1)} collective-permute-done((f32[16,256]{1,0:T(8,128)S(1)}, f32[16,256]{1,0:T(8,128)S(1)}, u32[]{:S(2)}, u32[]{:S(2)}) %collective-permute-start) | collective-permute-done | bytes 16416 | tf_op jit(solution)/shard_map/ppermute | solution.py:531
  28.9 6.6 %all-to-all-done = f32[128,13,1,128]{3,2,1,0:T(1,128)S(1)} async-done(((f32[128,13,1,128]{3,2,1,0:T(1,128)}), f32[128,13,1,128]{3,2,1,0:T(1,128)S(1)}, u32[]{:S(2)}, u32[]{:S(2)}) %all-to-all-start) | async-done | bytes 852000 | tf_op jit(solution)/shard_map/all_to_all | solution.py:524
  35.6 12.1 %pair.2.forces = f32[1536,128]{1,0:T(8,128)} custom-call(s32[2,256]{1,0:T(2,128)S(1)} %bitcast.24, f32[1664,128]{1,0:T(8,128)S(1)} %bitcast.20, f32[16,256]{1,0:T(8,128)S(1)} %collective-permute-done.col_a, f32[16,256]{1,0:T(8,128)S(1)} %collective-permute-done.1.col_b, f32[16,512]{1,0:T(8,128)S(1)} %collective-permute-done.2.row_a, ...), custom_call_target="tpu_custom_call" | custom-call | flops 2000000000 | bytes 2000000 | tf_op jit(solution)/shard_map/pair/pallas_call | solution.py:418
  47.6 4.9 %all-to-all-start.1 = ((f32[128,3,4,128]{3,2,1,0:T(4,128)}), f32[128,3,4,128]{3,2,1,0:T(4,128)}, u32[]{:S(2)}, u32[]{:S(2)}) async-start(f32[128,3,4,128]{3,2,1,0:T(4,128)} %bitcast.4), calls=%async_computation.1 | async-start | bytes 1572864 | tf_op jit(solution)/shard_map/all_to_all | solution.py:524
  53.2 11.8 %stencil.2.base = f32[3,1024,128]{2,1,0:T(8,128)} custom-call(s32[10]{0:T(128)} %stack.67.flags, f32[3,256,512]{2,1,0:T(8,128)} %x.5, f32[3,256,512]{2,1,0:T(8,128)} %velocity.1, f32[256,512]{1,0:T(8,128)} %stiffness.3, f32[16,256]{1,0:T(8,128)} %copy-done.7, f32[16,256]{1,0:T(8,128)} %copy-done.6, f32[16,512]{1,0:T(8,128)} %copy-done.3, ...), custom_call_target="tpu_custom_call" | custom-call | flops 20000000 | bytes 6000000 | tf_op jit(solution)/shard_map/stencil/pallas_call | solution.py:260
  65.0 4.1 %all-to-all-done.1 = f32[128,3,4,128]{3,2,1,0:T(4,128)} async-done(((f32[128,3,4,128]{3,2,1,0:T(4,128)}), f32[128,3,4,128]{3,2,1,0:T(4,128)}, u32[]{:S(2)}, u32[]{:S(2)}) %all-to-all-start.1) | async-done | bytes 786464 | tf_op jit(solution)/shard_map/all_to_all | solution.py:524
  69.1 7.4 %advance.2 = (f32[3,256,512]{2,1,0:T(8,128)}, f32[3,256,512]{2,1,0:T(8,128)}, f32[1664,128]{1,0:T(8,128)}, f32[16,256]{1,0:T(8,128)}, f32[16,512]{1,0:T(8,128)}) custom-call(s32[512]{0:T(512)} %bitcast.29, f32[1536,128]{1,0:T(8,128)} %bitcast.5.returned, f32[3,1024,128]{2,1,0:T(8,128)} %stencil.2.base, f32[3,256,512]{2,1,0:T(8,128)} %x.5), custom_call_target="tpu_custom_call" | custom-call | flops 2000000 | bytes 8000000 | tf_op jit(solution)/shard_map/advance/pallas_call | solution.py:502
  76.5 5.6 %all-to-all-start.2 = ((f32[128,13,1,128]{3,2,1,0:T(1,128)}), f32[128,13,1,128]{3,2,1,0:T(1,128)S(1)}, u32[]{:S(2)}, u32[]{:S(2)}) async-start(f32[128,13,1,128]{3,2,1,0:T(1,128)} %bitcast.26), calls=%async_computation.2 | async-start | bytes 1703936 | tf_op jit(solution)/shard_map/all_to_all | solution.py:524
  82.2 3.5 %collective-permute-start.7 = (f32[16,512]{1,0:T(8,128)S(1)}, f32[16,512]{1,0:T(8,128)S(1)}, u32[]{:S(2)}, u32[]{:S(2)}) collective-permute-start(f32[16,512]{1,0:T(8,128)S(1)} %copy-done.12), channel_id=1, source_target_pairs={{16,32},{32,16},{48,64},{64,48},{80,96},{96,80},{17,33},{33,17},{4... | collective-permute-start | bytes 98312 | tf_op jit(solution)/shard_map/ppermute | solution.py:531
  85.8 0.7 collective-permute-start.5
  86.5 3.7 %collective-permute-start.4 = (f32[16,256]{1,0:T(8,128)S(1)}, f32[16,256]{1,0:T(8,128)S(1)}, u32[]{:S(2)}, u32[]{:S(2)}) collective-permute-start(f32[16,256]{1,0:T(8,128)S(1)} %copy-done.14), channel_id=1, source_target_pairs={{0,1},{1,0},{2,3},{3,2},{4,5},{5,4},{6,7},{7,6},{8,9},{9,8},{10,11... | collective-permute-start | bytes 49160 | tf_op jit(solution)/shard_map/ppermute | solution.py:531
  90.2 2.8 %collective-permute-done.4.col_a = f32[16,256]{1,0:T(8,128)S(1)} collective-permute-done((f32[16,256]{1,0:T(8,128)S(1)}, f32[16,256]{1,0:T(8,128)S(1)}, u32[]{:S(2)}, u32[]{:S(2)}) %collective-permute-start.4) | collective-permute-done | bytes 16416 | tf_op jit(solution)/shard_map/ppermute | solution.py:531
  93.0 6.6 %all-to-all-done.2 = f32[128,13,1,128]{3,2,1,0:T(1,128)S(1)} async-done(((f32[128,13,1,128]{3,2,1,0:T(1,128)}), f32[128,13,1,128]{3,2,1,0:T(1,128)S(1)}, u32[]{:S(2)}, u32[]{:S(2)}) %all-to-all-start.2) | async-done | bytes 852000 | tf_op jit(solution)/shard_map/all_to_all | solution.py:524
  99.6 12.0 %pair.3.forces = f32[1536,128]{1,0:T(8,128)} custom-call(s32[2,256]{1,0:T(2,128)S(1)} %bitcast.25, f32[1664,128]{1,0:T(8,128)S(1)} %bitcast.22, f32[16,256]{1,0:T(8,128)S(1)} %collective-permute-done.4.col_a, f32[16,256]{1,0:T(8,128)S(1)} %collective-permute-done.5.col_b, f32[16,512]{1,0:T(8,128)S(1)} %collective-permute-done.6.row_a, ...), custom_call_target="tpu_custom_call" | custom-call | flops 2000000000 | bytes 2000000 | tf_op jit(solution)/shard_map/pair/pallas_call | solution.py:418
  111.7 4.9 %all-to-all-start.3 = ((f32[128,3,4,128]{3,2,1,0:T(4,128)}), f32[128,3,4,128]{3,2,1,0:T(4,128)}, u32[]{:S(2)}, u32[]{:S(2)}) async-start(f32[128,3,4,128]{3,2,1,0:T(4,128)} %bitcast.18), calls=%async_computation.3 | async-start | bytes 1572864 | tf_op jit(solution)/shard_map/all_to_all | solution.py:524
  116.6 11.9 %stencil.3.base = f32[3,1024,128]{2,1,0:T(8,128)} custom-call(s32[10]{0:T(128)} %stack.67.flags, f32[3,256,512]{2,1,0:T(8,128)} %get-tuple-element.18.x, f32[3,256,512]{2,1,0:T(8,128)} %get-tuple-element.19.velocity, f32[256,512]{1,0:T(8,128)} %stiffness.3, f32[16,256]{1,0:T(8,128)} %copy-done.9, f32[16,256]{1,0:T(8,128)} %copy-done.8, f32[16,512]{1,0:T(8,128)} %copy-done.5, ...), custom_call_target="tpu_custom_call" | custom-call | flops 20000000 | bytes 6000000 | tf_op jit(solution)/shard_map/stencil/pallas_call | solution.py:260
  128.5 4.7 %all-to-all-done.3 = f32[128,3,4,128]{3,2,1,0:T(4,128)} async-done(((f32[128,3,4,128]{3,2,1,0:T(4,128)}), f32[128,3,4,128]{3,2,1,0:T(4,128)}, u32[]{:S(2)}, u32[]{:S(2)}) %all-to-all-start.3) | async-done | bytes 786464 | tf_op jit(solution)/shard_map/all_to_all | solution.py:524
  133.2 6.1 %advance.3 = (f32[3,256,512]{2,1,0:T(8,128)}, f32[3,256,512]{2,1,0:T(8,128)}) custom-call(s32[512]{0:T(512)} %bitcast.30, f32[1536,128]{1,0:T(8,128)} %bitcast.19.returned, f32[3,1024,128]{2,1,0:T(8,128)} %stencil.3.base, f32[3,256,512]{2,1,0:T(8,128)} %get-tuple-element.18.x), custom_call_target="tpu_custom_call" | custom-call | flops 2000000 | bytes 8000000 | tf_op jit(solution)/shard_map/advance/pallas_call | solution.py:502
  (41 shorter events, 0.9 us)
Async XLA Ops:
  6.5 15.2 %copy-start.15 = (f32[16,256]{1,0:T(8,128)S(1)}, f32[16,256]{1,0:T(8,128)}, u32[]{:S(2)}) copy-start(f32[16,256]{1,0:T(8,128)} %get-tuple-element.13) | copy-start | bytes 49156
  6.6 29.0 %copy-start.10 = (s32[1,1,2,256]{3,2,1,0:T(2,128)S(1)}, s32[1,1,2,256]{3,2,1,0:T(2,128)}, u32[]{:S(2)}) copy-start(s32[1,1,2,256]{3,2,1,0:T(2,128)} %param.9) | copy-start | bytes 6148
  6.6 29.0 %all-to-all-start = ((f32[128,13,1,128]{3,2,1,0:T(1,128)}), f32[128,13,1,128]{3,2,1,0:T(1,128)S(1)}, u32[]{:S(2)}, u32[]{:S(2)}) async-start(f32[128,13,1,128]{3,2,1,0:T(1,128)} %bitcast.27), calls=%async_computation | async-start | bytes 1703936 | tf_op jit(solution)/shard_map/all_to_all | solution.py:524
  18.1 10.8 %collective-permute-start.3 = (f32[16,512]{1,0:T(8,128)S(1)}, f32[16,512]{1,0:T(8,128)S(1)}, u32[]{:S(2)}, u32[]{:S(2)}) collective-permute-start(f32[16,512]{1,0:T(8,128)S(1)} %copy-done.13), channel_id=1, source_target_pairs={{16,32},{32,16},{48,64},{64,48},{80,96},{96,80},{17,33},{33,17},{4... | collective-permute-start | bytes 98312 | tf_op jit(solution)/shard_map/ppermute | solution.py:531
  21.6 7.3 %collective-permute-start.2 = (f32[16,512]{1,0:T(8,128)S(1)}, f32[16,512]{1,0:T(8,128)S(1)}, u32[]{:S(2)}, u32[]{:S(2)}) collective-permute-start(f32[16,512]{1,0:T(8,128)S(1)} %copy-done.13), channel_id=1, source_target_pairs={{0,16},{16,0},{32,48},{48,32},{64,80},{80,64},{96,112},{112,96},{1... | collective-permute-start | bytes 98312 | tf_op jit(solution)/shard_map/ppermute | solution.py:531
  21.7 4.4 %collective-permute-start.1 = (f32[16,256]{1,0:T(8,128)S(1)}, f32[16,256]{1,0:T(8,128)S(1)}, u32[]{:S(2)}, u32[]{:S(2)}) collective-permute-start(f32[16,256]{1,0:T(8,128)S(1)} %copy-done.15), channel_id=1, source_target_pairs={{1,2},{2,1},{3,4},{4,3},{5,6},{6,5},{7,8},{8,7},{9,10},{10,9},{11,... | collective-permute-start | bytes 49160 | tf_op jit(solution)/shard_map/ppermute | solution.py:531
  22.4 6.5 %collective-permute-start = (f32[16,256]{1,0:T(8,128)S(1)}, f32[16,256]{1,0:T(8,128)S(1)}, u32[]{:S(2)}, u32[]{:S(2)}) collective-permute-start(f32[16,256]{1,0:T(8,128)S(1)} %copy-done.15), channel_id=1, source_target_pairs={{0,1},{1,0},{2,3},{3,2},{4,5},{5,4},{6,7},{7,6},{8,9},{9,8},{10,11... | collective-permute-start | bytes 49160 | tf_op jit(solution)/shard_map/ppermute | solution.py:531
  26.1 21.5 %copy-start.6 = (f32[16,256]{1,0:T(8,128)}, f32[16,256]{1,0:T(8,128)S(1)}, u32[]{:S(2)}) copy-start(f32[16,256]{1,0:T(8,128)S(1)} %collective-permute-done.1.col_b) | copy-start | bytes 49156
  28.9 18.7 %copy-start.7 = (f32[16,256]{1,0:T(8,128)}, f32[16,256]{1,0:T(8,128)S(1)}, u32[]{:S(2)}) copy-start(f32[16,256]{1,0:T(8,128)S(1)} %collective-permute-done.col_a) | copy-start | bytes 49156
  28.9 18.7 %copy-start.2 = (f32[16,512]{1,0:T(8,128)}, f32[16,512]{1,0:T(8,128)S(1)}, u32[]{:S(2)}) copy-start(f32[16,512]{1,0:T(8,128)S(1)} %collective-permute-done.3.row_b) | copy-start | bytes 98308
  28.9 18.7 %copy-start.3 = (f32[16,512]{1,0:T(8,128)}, f32[16,512]{1,0:T(8,128)S(1)}, u32[]{:S(2)}) copy-start(f32[16,512]{1,0:T(8,128)S(1)} %collective-permute-done.2.row_a) | copy-start | bytes 98308
  35.6 12.1 %copy-start = (f32[128,13,1,128]{3,2,1,0:T(1,128)}, f32[128,13,1,128]{3,2,1,0:T(1,128)S(1)}, u32[]{:S(2)}) copy-start(f32[128,13,1,128]{3,2,1,0:T(1,128)S(1)} %all-to-all-done) | copy-start | bytes 2555908
  47.6 21.5 %all-to-all-start.1 = ((f32[128,3,4,128]{3,2,1,0:T(4,128)}), f32[128,3,4,128]{3,2,1,0:T(4,128)}, u32[]{:S(2)}, u32[]{:S(2)}) async-start(f32[128,3,4,128]{3,2,1,0:T(4,128)} %bitcast.4), calls=%async_computation.1 | async-start | bytes 1572864 | tf_op jit(solution)/shard_map/all_to_all | solution.py:524
  76.5 23.1 %copy-start.11 = (s32[1,1,2,256]{3,2,1,0:T(2,128)S(1)}, s32[1,1,2,256]{3,2,1,0:T(2,128)}, u32[]{:S(2)}) copy-start(s32[1,1,2,256]{3,2,1,0:T(2,128)} %param.9) | copy-start | bytes 6148
  76.5 23.1 %all-to-all-start.2 = ((f32[128,13,1,128]{3,2,1,0:T(1,128)}), f32[128,13,1,128]{3,2,1,0:T(1,128)S(1)}, u32[]{:S(2)}, u32[]{:S(2)}) async-start(f32[128,13,1,128]{3,2,1,0:T(1,128)} %bitcast.26), calls=%async_computation.2 | async-start | bytes 1703936 | tf_op jit(solution)/shard_map/all_to_all | solution.py:524
  82.2 10.8 %collective-permute-start.7 = (f32[16,512]{1,0:T(8,128)S(1)}, f32[16,512]{1,0:T(8,128)S(1)}, u32[]{:S(2)}, u32[]{:S(2)}) collective-permute-start(f32[16,512]{1,0:T(8,128)S(1)} %copy-done.12), channel_id=1, source_target_pairs={{16,32},{32,16},{48,64},{64,48},{80,96},{96,80},{17,33},{33,17},{4... | collective-permute-start | bytes 98312 | tf_op jit(solution)/shard_map/ppermute | solution.py:531
  85.7 7.3 %collective-permute-start.6 = (f32[16,512]{1,0:T(8,128)S(1)}, f32[16,512]{1,0:T(8,128)S(1)}, u32[]{:S(2)}, u32[]{:S(2)}) collective-permute-start(f32[16,512]{1,0:T(8,128)S(1)} %copy-done.12), channel_id=1, source_target_pairs={{0,16},{16,0},{32,48},{48,32},{64,80},{80,64},{96,112},{112,96},{1... | collective-permute-start | bytes 98312 | tf_op jit(solution)/shard_map/ppermute | solution.py:531
  85.8 4.4 %collective-permute-start.5 = (f32[16,256]{1,0:T(8,128)S(1)}, f32[16,256]{1,0:T(8,128)S(1)}, u32[]{:S(2)}, u32[]{:S(2)}) collective-permute-start(f32[16,256]{1,0:T(8,128)S(1)} %copy-done.14), channel_id=1, source_target_pairs={{1,2},{2,1},{3,4},{4,3},{5,6},{6,5},{7,8},{8,7},{9,10},{10,9},{11,... | collective-permute-start | bytes 49160 | tf_op jit(solution)/shard_map/ppermute | solution.py:531
  86.5 6.5 %collective-permute-start.4 = (f32[16,256]{1,0:T(8,128)S(1)}, f32[16,256]{1,0:T(8,128)S(1)}, u32[]{:S(2)}, u32[]{:S(2)}) collective-permute-start(f32[16,256]{1,0:T(8,128)S(1)} %copy-done.14), channel_id=1, source_target_pairs={{0,1},{1,0},{2,3},{3,2},{4,5},{5,4},{6,7},{7,6},{8,9},{9,8},{10,11... | collective-permute-start | bytes 49160 | tf_op jit(solution)/shard_map/ppermute | solution.py:531
  90.2 21.5 %copy-start.8 = (f32[16,256]{1,0:T(8,128)}, f32[16,256]{1,0:T(8,128)S(1)}, u32[]{:S(2)}) copy-start(f32[16,256]{1,0:T(8,128)S(1)} %collective-permute-done.5.col_b) | copy-start | bytes 49156
  93.0 18.7 %copy-start.9 = (f32[16,256]{1,0:T(8,128)}, f32[16,256]{1,0:T(8,128)S(1)}, u32[]{:S(2)}) copy-start(f32[16,256]{1,0:T(8,128)S(1)} %collective-permute-done.4.col_a) | copy-start | bytes 49156
  93.0 18.7 %copy-start.4 = (f32[16,512]{1,0:T(8,128)}, f32[16,512]{1,0:T(8,128)S(1)}, u32[]{:S(2)}) copy-start(f32[16,512]{1,0:T(8,128)S(1)} %collective-permute-done.7.row_b) | copy-start | bytes 98308
  93.0 18.7 %copy-start.5 = (f32[16,512]{1,0:T(8,128)}, f32[16,512]{1,0:T(8,128)S(1)}, u32[]{:S(2)}) copy-start(f32[16,512]{1,0:T(8,128)S(1)} %collective-permute-done.6.row_a) | copy-start | bytes 98308
  111.7 21.5 %all-to-all-start.3 = ((f32[128,3,4,128]{3,2,1,0:T(4,128)}), f32[128,3,4,128]{3,2,1,0:T(4,128)}, u32[]{:S(2)}, u32[]{:S(2)}) async-start(f32[128,3,4,128]{3,2,1,0:T(4,128)} %bitcast.18), calls=%async_computation.3 | async-start | bytes 1572864 | tf_op jit(solution)/shard_map/all_to_all | solution.py:524
  (4 other events, 38.5 us)

commit v2 on v1

--- a/solution.py
+++ b/solution.py
@@ -37,11 +37,11 @@
 ROOM = pltpu.CompilerParams(vmem_limit_bytes=40 * 2**20)
 
 
-def pack_tiles(route, held, sent, corners):
+def pack_tiles(row_of, count, held, sent, corners):
     def body(step, carry):
         for u in range(8):
             slot = step * 8 + u
-            row = route[slot]
+            row = row_of(slot)
             to = (step * 2 + u // SLOTS) * BLOCK + (u % SLOTS) * 3
             for c in range(3):
                 sent[pl.ds(to + c, 1), :] = held[c, pl.ds(row, 1), :]
@@ -49,7 +49,7 @@
             sent[pl.ds((step * 2 + u) * BLOCK + BLOCK - 1, 1), :] = corners
         return carry
 
-    lax.fori_loop(0, route.shape[0] // 8, body, 0)
+    lax.fori_loop(0, count // 8, body, 0)
 
 
 def pack_edges(held, cols, rows_out, rows):
@@ -86,7 +86,7 @@
     return copies
 
 
-def pack_kernel(route, x, sent, cols, rows_out, held, sems):
+def pack_kernel(tiles, x, sent, cols, rows_out, held, sems):
     rows = x.shape[1]
     copies = block_copies(x, lambda c, b: held.at[c, pl.ds(b * rows, rows), :], sems, rows)
     for copy in copies:
@@ -94,7 +94,13 @@
     for copy in copies:
         copy.wait()
     corners = pack_edges(held, cols, rows_out, rows)
-    pack_tiles(route, held, sent, corners)
+    blocks = x.shape[2] // TILE
+
+    def row_of(slot):
+        tile = jnp.maximum(tiles[slot], 0)
+        return lax.rem(tile, blocks) * rows + lax.div(tile, blocks)
+
+    pack_tiles(row_of, tiles.shape[0], held, sent, corners)
 
 
 def blocked(shape):
@@ -201,7 +207,7 @@
                 curve[c, b, pl.ds(at, 8), :] = value
         return carry
 
-    lax.fori_loop(0, rows // 8 + 2, bend_tile, 0, unroll=2)
+    lax.fori_loop(0, rows // 8 + 2, bend_tile, 0, unroll=17)
     keep_above = jnp.where(flags[0] > 0, 0.0, 1.0)
     keep_below = jnp.where(flags[1] > 0, 0.0, 1.0)
     for c in range(3):
@@ -251,7 +257,7 @@
                 base[c, pl.ds(at + (b - 1) * rows, 8), :] = was + time_step * (force - damping * was)
         return carry
 
-    lax.fori_loop(0, rows // 8, force_tile, 0, unroll=2)
+    lax.fori_loop(0, rows // 8, force_tile, 0, unroll=8)
 
 
 def stencil(flags, x, velocity, stiffness, col_a, col_b, row_a, row_b, received, forces):
@@ -308,7 +314,7 @@
                     q[pl.ds(at + r + 4, 8, stride=8), :] = part
         return carry
 
-    lax.fori_loop(0, owners // 8, prepare, 0)
+    lax.fori_loop(0, owners // 8, prepare, 0, unroll=4)
 
     def tile_at(slot):
         return pl.multiple_of((lax.rem(slot, SLOTS) * owners + lax.div(slot, SLOTS)) * 8, 8)
@@ -410,7 +416,7 @@
                 out[to, :] = near * total - at(c) * (1.0 / SCALE)
         return carry
 
-    lax.fori_loop(0, owners // 8, finish, 0)
+    lax.fori_loop(0, owners // 8, finish, 0, unroll=4)
 
 
 def pair_forces(pairs, received, col_a, col_b, row_a, row_b):
@@ -450,11 +456,13 @@
     arrive = pltpu.make_async_copy(returned, incoming, more.at[0])
     begin = pltpu.make_async_copy(base, start, more.at[1])
     places = block_copies(x, block(held), sems, rows)
-    for copy in (arrive, begin, *places):
-        copy.start()
+    arrive.start()
+    begin.start()
     even[...] = jnp.zeros_like(even)
     odd[...] = jnp.zeros_like(odd)
     arrive.wait()
+    for copy in places:
+        copy.start()
 
     def scatter(step, carry):
         for u in range(4):
@@ -467,13 +475,13 @@
 
     lax.fori_loop(0, route.shape[0] // 8, scatter, 0)
     begin.wait()
-    for copy in places:
-        copy.wait()
     leave = block_copies(speed, block(even), outs.at[0], rows, True)
     leave += block_copies(place, block(held), outs.at[1], rows, True)
     half = len(leave) // 2
     for c in range(3):
         for b in range(blocks):
+
+            places[c * blocks + b].wait()
 
             def move(t, carry):
                 inner = pl.ds(pl.multiple_of(t * 8, 8) + b * rows, 8)
@@ -487,7 +495,7 @@
             leave[half + c * blocks + b].start()
     if not last:
         corners = pack_edges(held, cols, rows_out, rows)
-        pack_tiles(route, held, sent, corners)
+        pack_tiles(lambda slot: route[slot], route.shape[0], held, sent, corners)
     for copy in leave:
         copy.wait()
 
@@ -532,7 +540,8 @@
 
 
 def local(positions, velocity, stiffness, send_tiles, pair_tiles):
-    tile = jnp.maximum(send_tiles.reshape(-1), 0)
+    named = send_tiles.reshape(-1)
+    tile = jnp.maximum(named, 0)
     blocks = positions.shape[2] // TILE
     route = lax.rem(tile, blocks) * positions.shape[1] + lax.div(tile, blocks)
     paired = pair_tiles.reshape(2, -1)
@@ -545,7 +554,7 @@
             for i, j in near
         ]
     ).astype(jnp.int32)
-    sent, cols, rows = pack(route, positions)
+    sent, cols, rows = pack(named, positions)
     for repeat in range(STEPS):
         received = exchange(sent)
         col_a, col_b = swap(cols, "gy")

time: 140 us -> 138 us (0.986)
  Pallas kernels: 65.9 us -> 62 us
  waiting for transfers between devices: 27.7 us -> 29.7 us
    pallas_call x2, Pallas kernels: 23.7 us -> 20.8 us  [stencil(): pl.pallas_call(stencil_kernel, out_shape=jax.ShapeDtypeStruct(blocked(x.s...]
    all_to_all x4, waiting for transfers between devices: 22 us -> 24.3 us  [exchange(): lax.all_to_all(shaped, ('gx', 'gy'), split_axis=0, concat_axis=0, tiled=T...]
  transfers between devices with their start and end apart: 12 -> 12, of which waited for: 6 -> 6; matrix products, arithmetic and copies ran while one was open for 0% -> 1% of each run, Pallas kernels for 17% -> 15%
where the time goes in v2:
time: 138 us; the launch traced here: 137 us
  Pallas kernels  62 us (45%)
  starting transfers between devices  42.7 us (31%)
  waiting for transfers between devices  29.7 us (22%)
    all_to_all x4, starting transfers between devices, exchange(): lax.all_to_all(shaped, ('gx', 'gy'), split_axis=0, concat_axis=0, tiled=T...  26.6 us
    all_to_all x4, waiting for transfers between devices, exchange(): lax.all_to_all(shaped, ('gx', 'gy'), split_axis=0, concat_axis=0, tiled=T...  24.3 us
    pallas_call x2, Pallas kernels, pair_forces(): pl.pallas_call(pair_kernel, out_shape=jax.ShapeDtypeStruct((slots * 3, TI...  23.9 us
    pallas_call x2, Pallas kernels, stencil(): pl.pallas_call(stencil_kernel, out_shape=jax.ShapeDtypeStruct(blocked(x.s...  20.8 us
    ppermute x8, starting transfers between devices, swap(): return [lax.ppermute(value, axis, pairs) for pairs in both]  16.1 us
    pallas_call x2, Pallas kernels, advance(): pl.pallas_call(functools.partial(advance_kernel, last), out_shape=shapes,...  12.4 us
    ppermute x8, waiting for transfers between devices, swap(): return [lax.ppermute(value, axis, pairs) for pairs in both]  5.44 us
    pallas_call x1, Pallas kernels, pack(): pl.pallas_call(pack_kernel, out_shape=packed_shapes(route, x), in_specs=[...  4.95 us
  transfers between devices with their start and end apart: 12, of which 6 were waited for; matrix products, arithmetic and copies ran while one was open for 1% of the time, Pallas kernels for 15%

profile of v2, /device:TPU:1, one launch (start us, length us, event | category | flops | bytes accessed | tf_op | source)
XLA Modules:
  0.0 136.9 jit_solution(4763689424447530377)
XLA Ops:
  0.6 5.0 %pack.1 = (f32[1664,128]{1,0:T(8,128)}, f32[16,256]{1,0:T(8,128)}, f32[16,512]{1,0:T(8,128)}) custom-call(s32[512]{0:T(512)} %bitcast.28, f32[3,256,512]{2,1,0:T(8,128)} %x.5), custom_call_target="tpu_custom_call" | custom-call | flops 400000 | bytes 3000000 | tf_op jit(solution)/shard_map/pack/pallas_call | solution.py:120
  5.6 11.5 %all-to-all-start = ((f32[128,13,1,128]{3,2,1,0:T(1,128)}), f32[128,13,1,128]{3,2,1,0:T(1,128)S(1)}, u32[]{:S(2)}, u32[]{:S(2)}) async-start(f32[128,13,1,128]{3,2,1,0:T(1,128)} %bitcast.27), calls=%async_computation | async-start | bytes 1703936 | tf_op jit(solution)/shard_map/all_to_all | solution.py:532
  17.1 3.5 %collective-permute-start.3 = (f32[16,512]{1,0:T(8,128)S(1)}, f32[16,512]{1,0:T(8,128)S(1)}, u32[]{:S(2)}, u32[]{:S(2)}) collective-permute-start(f32[16,512]{1,0:T(8,128)S(1)} %copy-done.14), channel_id=1, source_target_pairs={{16,32},{32,16},{48,64},{64,48},{80,96},{96,80},{17,33},{33,17},{4... | collective-permute-start | bytes 98312 | tf_op jit(solution)/shard_map/ppermute | solution.py:539
  20.8 0.7 collective-permute-start.1
  21.5 3.7 %collective-permute-start = (f32[16,256]{1,0:T(8,128)S(1)}, f32[16,256]{1,0:T(8,128)S(1)}, u32[]{:S(2)}, u32[]{:S(2)}) collective-permute-start(f32[16,256]{1,0:T(8,128)S(1)} %copy-done.16), channel_id=1, source_target_pairs={{0,1},{1,0},{2,3},{3,2},{4,5},{5,4},{6,7},{7,6},{8,9},{9,8},{10,11... | collective-permute-start | bytes 49160 | tf_op jit(solution)/shard_map/ppermute | solution.py:539
  25.2 2.8 %collective-permute-done.col_a = f32[16,256]{1,0:T(8,128)S(1)} collective-permute-done((f32[16,256]{1,0:T(8,128)S(1)}, f32[16,256]{1,0:T(8,128)S(1)}, u32[]{:S(2)}, u32[]{:S(2)}) %collective-permute-start) | collective-permute-done | bytes 16416 | tf_op jit(solution)/shard_map/ppermute | solution.py:539
  28.0 6.6 %all-to-all-done = f32[128,13,1,128]{3,2,1,0:T(1,128)S(1)} async-done(((f32[128,13,1,128]{3,2,1,0:T(1,128)}), f32[128,13,1,128]{3,2,1,0:T(1,128)S(1)}, u32[]{:S(2)}, u32[]{:S(2)}) %all-to-all-start) | async-done | bytes 852000 | tf_op jit(solution)/shard_map/all_to_all | solution.py:532
  34.6 11.9 %pair.2.forces = f32[1536,128]{1,0:T(8,128)} custom-call(s32[2,256]{1,0:T(2,128)S(1)} %bitcast.24, f32[1664,128]{1,0:T(8,128)S(1)} %bitcast.20, f32[16,256]{1,0:T(8,128)S(1)} %collective-permute-done.col_a, f32[16,256]{1,0:T(8,128)S(1)} %collective-permute-done.1.col_b, f32[16,512]{1,0:T(8,128)S(1)} %collective-permute-done.2.row_a, ...), custom_call_target="tpu_custom_call" | custom-call | flops 2000000000 | bytes 2000000 | tf_op jit(solution)/shard_map/pair/pallas_call | solution.py:424
  46.6 5.2 %all-to-all-start.1 = ((f32[128,3,4,128]{3,2,1,0:T(4,128)}), f32[128,3,4,128]{3,2,1,0:T(4,128)}, u32[]{:S(2)}, u32[]{:S(2)}) async-start(f32[128,3,4,128]{3,2,1,0:T(4,128)} %bitcast.4), calls=%async_computation.1 | async-start | bytes 1572864 | tf_op jit(solution)/shard_map/all_to_all | solution.py:532
  51.8 0.7 stack.67.flags
  53.1 10.3 %stencil.2.base = f32[3,1024,128]{2,1,0:T(8,128)} custom-call(s32[10]{0:T(128)} %stack.67.flags, f32[3,256,512]{2,1,0:T(8,128)} %x.5, f32[3,256,512]{2,1,0:T(8,128)} %velocity.1, f32[256,512]{1,0:T(8,128)} %stiffness.3, f32[16,256]{1,0:T(8,128)} %copy-done.7, f32[16,256]{1,0:T(8,128)} %copy-done.6, f32[16,512]{1,0:T(8,128)} %copy-done.3, ...), custom_call_target="tpu_custom_call" | custom-call | flops 20000000 | bytes 6000000 | tf_op jit(solution)/shard_map/stencil/pallas_call | solution.py:266
  63.4 4.9 %all-to-all-done.1 = f32[128,3,4,128]{3,2,1,0:T(4,128)} async-done(((f32[128,3,4,128]{3,2,1,0:T(4,128)}), f32[128,3,4,128]{3,2,1,0:T(4,128)}, u32[]{:S(2)}, u32[]{:S(2)}) %all-to-all-start.1) | async-done | bytes 786464 | tf_op jit(solution)/shard_map/all_to_all | solution.py:532
  68.3 6.9 %advance.2 = (f32[3,256,512]{2,1,0:T(8,128)}, f32[3,256,512]{2,1,0:T(8,128)}, f32[1664,128]{1,0:T(8,128)}, f32[16,256]{1,0:T(8,128)}, f32[16,512]{1,0:T(8,128)}) custom-call(s32[512]{0:T(512)} %shift-right-logical_add_fusion.route, f32[1536,128]{1,0:T(8,128)} %bitcast.5.returned, f32[3,1024,128]{2,1,0:T(8,128)} %stencil.2.base, f32[3,256,512]{2,1,0:T(8,128)} %x.5), custom_call_target="tpu_custom_call" | custom-call | flops 2000000 | bytes 8000000 | tf_op jit(solution)/shard_map/advance/pallas_call | solution.py:510
  75.3 4.8 %all-to-all-start.2 = ((f32[128,13,1,128]{3,2,1,0:T(1,128)}), f32[128,13,1,128]{3,2,1,0:T(1,128)S(1)}, u32[]{:S(2)}, u32[]{:S(2)}) async-start(f32[128,13,1,128]{3,2,1,0:T(1,128)} %bitcast.26), calls=%async_computation.2 | async-start | bytes 1703936 | tf_op jit(solution)/shard_map/all_to_all | solution.py:532
  80.1 3.5 %collective-permute-start.7 = (f32[16,512]{1,0:T(8,128)S(1)}, f32[16,512]{1,0:T(8,128)S(1)}, u32[]{:S(2)}, u32[]{:S(2)}) collective-permute-start(f32[16,512]{1,0:T(8,128)S(1)} %copy-done.13), channel_id=1, source_target_pairs={{16,32},{32,16},{48,64},{64,48},{80,96},{96,80},{17,33},{33,17},{4... | collective-permute-start | bytes 98312 | tf_op jit(solution)/shard_map/ppermute | solution.py:539
  83.7 0.7 collective-permute-start.5
  84.4 3.9 %collective-permute-start.4 = (f32[16,256]{1,0:T(8,128)S(1)}, f32[16,256]{1,0:T(8,128)S(1)}, u32[]{:S(2)}, u32[]{:S(2)}) collective-permute-start(f32[16,256]{1,0:T(8,128)S(1)} %copy-done.15), channel_id=1, source_target_pairs={{0,1},{1,0},{2,3},{3,2},{4,5},{5,4},{6,7},{7,6},{8,9},{9,8},{10,11... | collective-permute-start | bytes 49160 | tf_op jit(solution)/shard_map/ppermute | solution.py:539
  88.3 2.6 %collective-permute-done.4.col_a = f32[16,256]{1,0:T(8,128)S(1)} collective-permute-done((f32[16,256]{1,0:T(8,128)S(1)}, f32[16,256]{1,0:T(8,128)S(1)}, u32[]{:S(2)}, u32[]{:S(2)}) %collective-permute-start.4) | collective-permute-done | bytes 16416 | tf_op jit(solution)/shard_map/ppermute | solution.py:539
  90.9 6.6 %all-to-all-done.2 = f32[128,13,1,128]{3,2,1,0:T(1,128)S(1)} async-done(((f32[128,13,1,128]{3,2,1,0:T(1,128)}), f32[128,13,1,128]{3,2,1,0:T(1,128)S(1)}, u32[]{:S(2)}, u32[]{:S(2)}) %all-to-all-start.2) | async-done | bytes 852000 | tf_op jit(solution)/shard_map/all_to_all | solution.py:532
  97.5 11.9 %pair.3.forces = f32[1536,128]{1,0:T(8,128)} custom-call(s32[2,256]{1,0:T(2,128)S(1)} %bitcast.25, f32[1664,128]{1,0:T(8,128)S(1)} %bitcast.22, f32[16,256]{1,0:T(8,128)S(1)} %collective-permute-done.4.col_a, f32[16,256]{1,0:T(8,128)S(1)} %collective-permute-done.5.col_b, f32[16,512]{1,0:T(8,128)S(1)} %collective-permute-done.6.row_a, ...), custom_call_target="tpu_custom_call" | custom-call | flops 2000000000 | bytes 2000000 | tf_op jit(solution)/shard_map/pair/pallas_call | solution.py:424
  109.5 5.2 %all-to-all-start.3 = ((f32[128,3,4,128]{3,2,1,0:T(4,128)}), f32[128,3,4,128]{3,2,1,0:T(4,128)}, u32[]{:S(2)}, u32[]{:S(2)}) async-start(f32[128,3,4,128]{3,2,1,0:T(4,128)} %bitcast.18), calls=%async_computation.3 | async-start | bytes 1572864 | tf_op jit(solution)/shard_map/all_to_all | solution.py:532
  114.7 10.5 %stencil.3.base = f32[3,1024,128]{2,1,0:T(8,128)} custom-call(s32[10]{0:T(128)} %stack.67.flags, f32[3,256,512]{2,1,0:T(8,128)} %get-tuple-element.18.x, f32[3,256,512]{2,1,0:T(8,128)} %get-tuple-element.19.velocity, f32[256,512]{1,0:T(8,128)} %stiffness.3, f32[16,256]{1,0:T(8,128)} %copy-done.9, f32[16,256]{1,0:T(8,128)} %copy-done.8, f32[16,512]{1,0:T(8,128)} %copy-done.5, ...), custom_call_target="tpu_custom_call" | custom-call | flops 20000000 | bytes 6000000 | tf_op jit(solution)/shard_map/stencil/pallas_call | solution.py:266
  125.2 6.1 %all-to-all-done.3 = f32[128,3,4,128]{3,2,1,0:T(4,128)} async-done(((f32[128,3,4,128]{3,2,1,0:T(4,128)}), f32[128,3,4,128]{3,2,1,0:T(4,128)}, u32[]{:S(2)}, u32[]{:S(2)}) %all-to-all-start.3) | async-done | bytes 786464 | tf_op jit(solution)/shard_map/all_to_all | solution.py:532
  131.3 5.5 %advance.3 = (f32[3,256,512]{2,1,0:T(8,128)}, f32[3,256,512]{2,1,0:T(8,128)}) custom-call(s32[512]{0:T(512)} %shift-right-logical_add_fusion.route, f32[1536,128]{1,0:T(8,128)} %bitcast.19.returned, f32[3,1024,128]{2,1,0:T(8,128)} %stencil.3.base, f32[3,256,512]{2,1,0:T(8,128)} %get-tuple-element.18.x), custom_call_target="tpu_custom_call" | custom-call | flops 2000000 | bytes 8000000 | tf_op jit(solution)/shard_map/advance/pallas_call | solution.py:510
  (43 shorter events, 0.9 us)
Async XLA Ops:
  5.6 15.2 %copy-start.16 = (f32[16,256]{1,0:T(8,128)S(1)}, f32[16,256]{1,0:T(8,128)}, u32[]{:S(2)}) copy-start(f32[16,256]{1,0:T(8,128)} %get-tuple-element.13) | copy-start | bytes 49156
  5.6 29.0 %copy-start.10 = (s32[1,1,2,256]{3,2,1,0:T(2,128)S(1)}, s32[1,1,2,256]{3,2,1,0:T(2,128)}, u32[]{:S(2)}) copy-start(s32[1,1,2,256]{3,2,1,0:T(2,128)} %param.9) | copy-start | bytes 6148
  5.6 29.0 %all-to-all-start = ((f32[128,13,1,128]{3,2,1,0:T(1,128)}), f32[128,13,1,128]{3,2,1,0:T(1,128)S(1)}, u32[]{:S(2)}, u32[]{:S(2)}) async-start(f32[128,13,1,128]{3,2,1,0:T(1,128)} %bitcast.27), calls=%async_computation | async-start | bytes 1703936 | tf_op jit(solution)/shard_map/all_to_all | solution.py:532
  17.1 10.8 %collective-permute-start.3 = (f32[16,512]{1,0:T(8,128)S(1)}, f32[16,512]{1,0:T(8,128)S(1)}, u32[]{:S(2)}, u32[]{:S(2)}) collective-permute-start(f32[16,512]{1,0:T(8,128)S(1)} %copy-done.14), channel_id=1, source_target_pairs={{16,32},{32,16},{48,64},{64,48},{80,96},{96,80},{17,33},{33,17},{4... | collective-permute-start | bytes 98312 | tf_op jit(solution)/shard_map/ppermute | solution.py:539
  20.7 7.3 %collective-permute-start.2 = (f32[16,512]{1,0:T(8,128)S(1)}, f32[16,512]{1,0:T(8,128)S(1)}, u32[]{:S(2)}, u32[]{:S(2)}) collective-permute-start(f32[16,512]{1,0:T(8,128)S(1)} %copy-done.14), channel_id=1, source_target_pairs={{0,16},{16,0},{32,48},{48,32},{64,80},{80,64},{96,112},{112,96},{1... | collective-permute-start | bytes 98312 | tf_op jit(solution)/shard_map/ppermute | solution.py:539
  20.8 4.4 %collective-permute-start.1 = (f32[16,256]{1,0:T(8,128)S(1)}, f32[16,256]{1,0:T(8,128)S(1)}, u32[]{:S(2)}, u32[]{:S(2)}) collective-permute-start(f32[16,256]{1,0:T(8,128)S(1)} %copy-done.16), channel_id=1, source_target_pairs={{1,2},{2,1},{3,4},{4,3},{5,6},{6,5},{7,8},{8,7},{9,10},{10,9},{11,... | collective-permute-start | bytes 49160 | tf_op jit(solution)/shard_map/ppermute | solution.py:539
  21.5 6.5 %collective-permute-start = (f32[16,256]{1,0:T(8,128)S(1)}, f32[16,256]{1,0:T(8,128)S(1)}, u32[]{:S(2)}, u32[]{:S(2)}) collective-permute-start(f32[16,256]{1,0:T(8,128)S(1)} %copy-done.16), channel_id=1, source_target_pairs={{0,1},{1,0},{2,3},{3,2},{4,5},{5,4},{6,7},{7,6},{8,9},{9,8},{10,11... | collective-permute-start | bytes 49160 | tf_op jit(solution)/shard_map/ppermute | solution.py:539
  25.2 21.4 %copy-start.6 = (f32[16,256]{1,0:T(8,128)}, f32[16,256]{1,0:T(8,128)S(1)}, u32[]{:S(2)}) copy-start(f32[16,256]{1,0:T(8,128)S(1)} %collective-permute-done.1.col_b) | copy-start | bytes 49156
  28.0 18.6 %copy-start.7 = (f32[16,256]{1,0:T(8,128)}, f32[16,256]{1,0:T(8,128)S(1)}, u32[]{:S(2)}) copy-start(f32[16,256]{1,0:T(8,128)S(1)} %collective-permute-done.col_a) | copy-start | bytes 49156
  28.0 18.6 %copy-start.2 = (f32[16,512]{1,0:T(8,128)}, f32[16,512]{1,0:T(8,128)S(1)}, u32[]{:S(2)}) copy-start(f32[16,512]{1,0:T(8,128)S(1)} %collective-permute-done.3.row_b) | copy-start | bytes 98308
  28.0 18.6 %copy-start.3 = (f32[16,512]{1,0:T(8,128)}, f32[16,512]{1,0:T(8,128)S(1)}, u32[]{:S(2)}) copy-start(f32[16,512]{1,0:T(8,128)S(1)} %collective-permute-done.2.row_a) | copy-start | bytes 98308
  34.6 12.0 %copy-start = (f32[128,13,1,128]{3,2,1,0:T(1,128)}, f32[128,13,1,128]{3,2,1,0:T(1,128)S(1)}, u32[]{:S(2)}) copy-start(f32[128,13,1,128]{3,2,1,0:T(1,128)S(1)} %all-to-all-done) | copy-start | bytes 2555908
  46.6 21.8 %all-to-all-start.1 = ((f32[128,3,4,128]{3,2,1,0:T(4,128)}), f32[128,3,4,128]{3,2,1,0:T(4,128)}, u32[]{:S(2)}, u32[]{:S(2)}) async-start(f32[128,3,4,128]{3,2,1,0:T(4,128)} %bitcast.4), calls=%async_computation.1 | async-start | bytes 1572864 | tf_op jit(solution)/shard_map/all_to_all | solution.py:532
  75.3 22.3 %copy-start.11 = (s32[1,1,2,256]{3,2,1,0:T(2,128)S(1)}, s32[1,1,2,256]{3,2,1,0:T(2,128)}, u32[]{:S(2)}) copy-start(s32[1,1,2,256]{3,2,1,0:T(2,128)} %param.9) | copy-start | bytes 6148
  75.3 22.2 %all-to-all-start.2 = ((f32[128,13,1,128]{3,2,1,0:T(1,128)}), f32[128,13,1,128]{3,2,1,0:T(1,128)S(1)}, u32[]{:S(2)}, u32[]{:S(2)}) async-start(f32[128,13,1,128]{3,2,1,0:T(1,128)} %bitcast.26), calls=%async_computation.2 | async-start | bytes 1703936 | tf_op jit(solution)/shard_map/all_to_all | solution.py:532
  80.1 10.8 %collective-permute-start.7 = (f32[16,512]{1,0:T(8,128)S(1)}, f32[16,512]{1,0:T(8,128)S(1)}, u32[]{:S(2)}, u32[]{:S(2)}) collective-permute-start(f32[16,512]{1,0:T(8,128)S(1)} %copy-done.13), channel_id=1, source_target_pairs={{16,32},{32,16},{48,64},{64,48},{80,96},{96,80},{17,33},{33,17},{4... | collective-permute-start | bytes 98312 | tf_op jit(solution)/shard_map/ppermute | solution.py:539
  83.6 7.3 %collective-permute-start.6 = (f32[16,512]{1,0:T(8,128)S(1)}, f32[16,512]{1,0:T(8,128)S(1)}, u32[]{:S(2)}, u32[]{:S(2)}) collective-permute-start(f32[16,512]{1,0:T(8,128)S(1)} %copy-done.13), channel_id=1, source_target_pairs={{0,16},{16,0},{32,48},{48,32},{64,80},{80,64},{96,112},{112,96},{1... | collective-permute-start | bytes 98312 | tf_op jit(solution)/shard_map/ppermute | solution.py:539
  83.7 4.5 %collective-permute-start.5 = (f32[16,256]{1,0:T(8,128)S(1)}, f32[16,256]{1,0:T(8,128)S(1)}, u32[]{:S(2)}, u32[]{:S(2)}) collective-permute-start(f32[16,256]{1,0:T(8,128)S(1)} %copy-done.15), channel_id=1, source_target_pairs={{1,2},{2,1},{3,4},{4,3},{5,6},{6,5},{7,8},{8,7},{9,10},{10,9},{11,... | collective-permute-start | bytes 49160 | tf_op jit(solution)/shard_map/ppermute | solution.py:539
  84.4 6.5 %collective-permute-start.4 = (f32[16,256]{1,0:T(8,128)S(1)}, f32[16,256]{1,0:T(8,128)S(1)}, u32[]{:S(2)}, u32[]{:S(2)}) collective-permute-start(f32[16,256]{1,0:T(8,128)S(1)} %copy-done.15), channel_id=1, source_target_pairs={{0,1},{1,0},{2,3},{3,2},{4,5},{5,4},{6,7},{7,6},{8,9},{9,8},{10,11... | collective-permute-start | bytes 49160 | tf_op jit(solution)/shard_map/ppermute | solution.py:539
  88.3 21.2 %copy-start.8 = (f32[16,256]{1,0:T(8,128)}, f32[16,256]{1,0:T(8,128)S(1)}, u32[]{:S(2)}) copy-start(f32[16,256]{1,0:T(8,128)S(1)} %collective-permute-done.5.col_b) | copy-start | bytes 49156
  90.9 18.6 %copy-start.9 = (f32[16,256]{1,0:T(8,128)}, f32[16,256]{1,0:T(8,128)S(1)}, u32[]{:S(2)}) copy-start(f32[16,256]{1,0:T(8,128)S(1)} %collective-permute-done.4.col_a) | copy-start | bytes 49156
  90.9 18.6 %copy-start.4 = (f32[16,512]{1,0:T(8,128)}, f32[16,512]{1,0:T(8,128)S(1)}, u32[]{:S(2)}) copy-start(f32[16,512]{1,0:T(8,128)S(1)} %collective-permute-done.7.row_b) | copy-start | bytes 98308
  90.9 18.6 %copy-start.5 = (f32[16,512]{1,0:T(8,128)}, f32[16,512]{1,0:T(8,128)S(1)}, u32[]{:S(2)}) copy-start(f32[16,512]{1,0:T(8,128)S(1)} %collective-permute-done.6.row_a) | copy-start | bytes 98308
  109.5 21.8 %all-to-all-start.3 = ((f32[128,3,4,128]{3,2,1,0:T(4,128)}), f32[128,3,4,128]{3,2,1,0:T(4,128)}, u32[]{:S(2)}, u32[]{:S(2)}) async-start(f32[128,3,4,128]{3,2,1,0:T(4,128)} %bitcast.18), calls=%async_computation.3 | async-start | bytes 1572864 | tf_op jit(solution)/shard_map/all_to_all | solution.py:532
  (5 other events, 42.6 us)

commit v3 on v2

--- a/solution.py
+++ b/solution.py
@@ -291,8 +291,7 @@
     return one, two, rest - two
 
 
-def pair_kernel(pairs, received, col_a, col_b, row_a, row_b, out, acc, q1, q2, q3, w0, w1, g0, g1):
-    count = pairs.shape[1]
+def pair_kernel(used, pairs, received, col_a, col_b, row_a, row_b, out, acc, q1, q2, q3, w0, w1, g0, g1):
     owners = received.shape[0] // BLOCK
     slots = owners * SLOTS
     sub = lax.broadcasted_iota(jnp.int32, (8, TILE), 0)
@@ -391,7 +390,8 @@
             split_one(queue.pop(0), u, wb)
         add_all(results)
 
-    steps = count // GROUP
+    rounds = jnp.maximum(lax.div(used[0] + 2 * GROUP - 1, 2 * GROUP), 1)
+    steps = 2 * rounds
     weigh(0, w0, g0)
 
     def body(t, carry):
@@ -399,7 +399,7 @@
         both(2 * t + 1, w1, g1, w0, g0)
         return carry
 
-    lax.fori_loop(0, steps // 2 - 1, body, 0)
+    lax.fori_loop(0, rounds - 1, body, 0)
     both(steps - 2, w0, g0, w1, g1)
     push(steps - 1, w1, g1)
 
@@ -419,12 +419,12 @@
     lax.fori_loop(0, owners // 8, finish, 0, unroll=4)
 
 
-def pair_forces(pairs, received, col_a, col_b, row_a, row_b):
+def pair_forces(used, pairs, received, col_a, col_b, row_a, row_b):
     slots = received.shape[0] // BLOCK * SLOTS
     return pl.pallas_call(
         pair_kernel,
         out_shape=jax.ShapeDtypeStruct((slots * 3, TILE), F32),
-        in_specs=[SMEM, VMEM, ANY, ANY, ANY, ANY],
+        in_specs=[SMEM, SMEM, VMEM, ANY, ANY, ANY, ANY],
         out_specs=VMEM,
         compiler_params=ROOM,
         scratch_shapes=[
@@ -439,7 +439,7 @@
         ],
         name="pair",
         cost_estimate=pl.CostEstimate(flops=2_000_000_000, bytes_accessed=2_000_000, transcendentals=8_000_000),
-    )(pairs, received, col_a, col_b, row_a, row_b)
+    )(used, pairs, received, col_a, col_b, row_a, row_b)
 
 
 def advance_kernel(last, route, returned, base, x, *refs):
@@ -545,6 +545,7 @@
     blocks = positions.shape[2] // TILE
     route = lax.rem(tile, blocks) * positions.shape[1] + lax.div(tile, blocks)
     paired = pair_tiles.reshape(2, -1)
+    used = jnp.sum(paired[0] >= 0, dtype=jnp.int32).reshape(1)
     row, col = lax.axis_index("gx"), lax.axis_index("gy")
     near = [(row + i, col + j) for i in (-1, 1) for j in (-1, 1)]
     flags = jnp.stack(
@@ -559,7 +560,7 @@
         received = exchange(sent)
         col_a, col_b = swap(cols, "gy")
         row_a, row_b = swap(rows, "gx")
-        forces = pair_forces(paired, received, col_a, col_b, row_a, row_b)
+        forces = pair_forces(used, paired, received, col_a, col_b, row_a, row_b)
         returned = exchange(forces)
         base = stencil(flags, positions, velocity, stiffness, col_a, col_b, row_a, row_b, received, forces)
         last = repeat == STEPS - 1

time: 138 us -> 136 us (0.986)
  waiting for transfers between devices: 29.7 us -> 26.6 us
    all_to_all x4, waiting for transfers between devices: 24.3 us -> 21.5 us  [exchange(): lax.all_to_all(shaped, ('gx', 'gy'), split_axis=0, concat_axis=0, tiled=T...]
  transfers between devices with their start and end apart: 12 -> 12, of which waited for: 6 -> 7; matrix products, arithmetic and copies ran while one was open for 1% -> 1% of each run, Pallas kernels for 15% -> 15%
where the time goes in v3:
time: 136 us; the launch traced here: 135 us
  Pallas kernels  62.8 us (46%)
  starting transfers between devices  42.1 us (31%)
  waiting for transfers between devices  26.6 us (20%)
    all_to_all x4, starting transfers between devices, exchange(): lax.all_to_all(shaped, ('gx', 'gy'), split_axis=0, concat_axis=0, tiled=T...  25.6 us
    pallas_call x2, Pallas kernels, pair_forces(): pl.pallas_call(pair_kernel, out_shape=jax.ShapeDtypeStruct((slots * 3, TI...  24.6 us
    all_to_all x4, waiting for transfers between devices, exchange(): lax.all_to_all(shaped, ('gx', 'gy'), split_axis=0, concat_axis=0, tiled=T...  21.5 us
    pallas_call x2, Pallas kernels, stencil(): pl.pallas_call(stencil_kernel, out_shape=jax.ShapeDtypeStruct(blocked(x.s...  20.8 us
    ppermute x8, starting transfers between devices, swap(): return [lax.ppermute(value, axis, pairs) for pairs in both]  16.5 us
    pallas_call x2, Pallas kernels, advance(): pl.pallas_call(functools.partial(advance_kernel, last), out_shape=shapes,...  12.5 us
    ppermute x8, waiting for transfers between devices, swap(): return [lax.ppermute(value, axis, pairs) for pairs in both]  5.11 us
    pallas_call x1, Pallas kernels, pack(): pl.pallas_call(pack_kernel, out_shape=packed_shapes(route, x), in_specs=[...  4.95 us
  transfers between devices with their start and end apart: 12, of which 7 were waited for; matrix products, arithmetic and copies ran while one was open for 1% of the time, Pallas kernels for 15%

profile of v3, /device:TPU:1, one launch (start us, length us, event | category | flops | bytes accessed | tf_op | source)
XLA Modules:
  0.0 134.6 jit_solution(890454715202220467)
XLA Ops:
  0.6 5.0 %pack.1 = (f32[1664,128]{1,0:T(8,128)}, f32[16,256]{1,0:T(8,128)}, f32[16,512]{1,0:T(8,128)}) custom-call(s32[512]{0:T(512)} %bitcast.29, f32[3,256,512]{2,1,0:T(8,128)} %x.5), custom_call_target="tpu_custom_call" | custom-call | flops 400000 | bytes 3000000 | tf_op jit(solution)/shard_map/pack/pallas_call | solution.py:120
  5.6 11.5 %all-to-all-start = ((f32[128,13,1,128]{3,2,1,0:T(1,128)}), f32[128,13,1,128]{3,2,1,0:T(1,128)S(1)}, u32[]{:S(2)}, u32[]{:S(2)}) async-start(f32[128,13,1,128]{3,2,1,0:T(1,128)} %bitcast.28), calls=%async_computation | async-start | bytes 1703936 | tf_op jit(solution)/shard_map/all_to_all | solution.py:532
  17.1 0.7 collective-permute-start.1
  17.8 3.9 %collective-permute-start = (f32[16,256]{1,0:T(8,128)S(1)}, f32[16,256]{1,0:T(8,128)S(1)}, u32[]{:S(2)}, u32[]{:S(2)}) collective-permute-start(f32[16,256]{1,0:T(8,128)S(1)} %copy-done.16), channel_id=1, source_target_pairs={{0,1},{1,0},{2,3},{3,2},{4,5},{5,4},{6,7},{7,6},{8,9},{9,8},{10,11... | collective-permute-start | bytes 49160 | tf_op jit(solution)/shard_map/ppermute | solution.py:539
  21.7 3.9 %collective-permute-start.3 = (f32[16,512]{1,0:T(8,128)S(1)}, f32[16,512]{1,0:T(8,128)S(1)}, u32[]{:S(2)}, u32[]{:S(2)}) collective-permute-start(f32[16,512]{1,0:T(8,128)S(1)} %copy-done.14), channel_id=1, source_target_pairs={{16,32},{32,16},{48,64},{64,48},{80,96},{96,80},{17,33},{33,17},{4... | collective-permute-start | bytes 98312 | tf_op jit(solution)/shard_map/ppermute | solution.py:539
  26.3 1.6 %collective-permute-done.col_a = f32[16,256]{1,0:T(8,128)S(1)} collective-permute-done((f32[16,256]{1,0:T(8,128)S(1)}, f32[16,256]{1,0:T(8,128)S(1)}, u32[]{:S(2)}, u32[]{:S(2)}) %collective-permute-start) | collective-permute-done | bytes 16416 | tf_op jit(solution)/shard_map/ppermute | solution.py:539
  28.0 0.7 collective-permute-done.3.row_b
  28.6 6.0 %all-to-all-done = f32[128,13,1,128]{3,2,1,0:T(1,128)S(1)} async-done(((f32[128,13,1,128]{3,2,1,0:T(1,128)}), f32[128,13,1,128]{3,2,1,0:T(1,128)S(1)}, u32[]{:S(2)}, u32[]{:S(2)}) %all-to-all-start) | async-done | bytes 852000 | tf_op jit(solution)/shard_map/all_to_all | solution.py:532
  34.6 12.2 %pair.2.forces = f32[1536,128]{1,0:T(8,128)} custom-call(s32[1]{0:T(128)} %bitcast.1.used, s32[2,256]{1,0:T(2,128)S(1)} %bitcast.25, f32[1664,128]{1,0:T(8,128)S(1)} %bitcast.21, f32[16,256]{1,0:T(8,128)S(1)} %collective-permute-done.col_a, f32[16,256]{1,0:T(8,128)S(1)} %collective-permute-done.1.col_b, f32[16,512]{1,0:T(8,128)S(1)} %collective-permute-done.2.row_a, ...), custom_call_target="tpu_custom_call" | custom-call | flops 2000000000 | bytes 2000000 | tf_op jit(solution)/shard_map/pair/pallas_call | solution.py:424
  46.9 4.6 %all-to-all-start.1 = ((f32[128,3,4,128]{3,2,1,0:T(4,128)}), f32[128,3,4,128]{3,2,1,0:T(4,128)}, u32[]{:S(2)}, u32[]{:S(2)}) async-start(f32[128,3,4,128]{3,2,1,0:T(4,128)} %bitcast.5), calls=%async_computation.1 | async-start | bytes 1572864 | tf_op jit(solution)/shard_map/all_to_all | solution.py:532
  51.6 0.7 stack.67.flags
  52.8 10.3 %stencil.2.base = f32[3,1024,128]{2,1,0:T(8,128)} custom-call(s32[10]{0:T(128)} %stack.67.flags, f32[3,256,512]{2,1,0:T(8,128)} %x.5, f32[3,256,512]{2,1,0:T(8,128)} %velocity.1, f32[256,512]{1,0:T(8,128)} %stiffness.3, f32[16,256]{1,0:T(8,128)} %copy-done.7, f32[16,256]{1,0:T(8,128)} %copy-done.6, f32[16,512]{1,0:T(8,128)} %copy-done.3, ...), custom_call_target="tpu_custom_call" | custom-call | flops 20000000 | bytes 6000000 | tf_op jit(solution)/shard_map/stencil/pallas_call | solution.py:266
  63.2 3.8 %all-to-all-done.1 = f32[128,3,4,128]{3,2,1,0:T(4,128)} async-done(((f32[128,3,4,128]{3,2,1,0:T(4,128)}), f32[128,3,4,128]{3,2,1,0:T(4,128)}, u32[]{:S(2)}, u32[]{:S(2)}) %all-to-all-start.1) | async-done | bytes 786464 | tf_op jit(solution)/shard_map/all_to_all | solution.py:532
  67.0 6.9 %advance.2 = (f32[3,256,512]{2,1,0:T(8,128)}, f32[3,256,512]{2,1,0:T(8,128)}, f32[1664,128]{1,0:T(8,128)}, f32[16,256]{1,0:T(8,128)}, f32[16,512]{1,0:T(8,128)}) custom-call(s32[512]{0:T(512)} %shift-right-logical_add_fusion.route, f32[1536,128]{1,0:T(8,128)} %bitcast.6.returned, f32[3,1024,128]{2,1,0:T(8,128)} %stencil.2.base, f32[3,256,512]{2,1,0:T(8,128)} %x.5), custom_call_target="tpu_custom_call" | custom-call | flops 2000000 | bytes 8000000 | tf_op jit(solution)/shard_map/advance/pallas_call | solution.py:510
  74.0 4.8 %all-to-all-start.2 = ((f32[128,13,1,128]{3,2,1,0:T(1,128)}), f32[128,13,1,128]{3,2,1,0:T(1,128)S(1)}, u32[]{:S(2)}, u32[]{:S(2)}) async-start(f32[128,13,1,128]{3,2,1,0:T(1,128)} %bitcast.27), calls=%async_computation.2 | async-start | bytes 1703936 | tf_op jit(solution)/shard_map/all_to_all | solution.py:532
  78.8 3.5 %collective-permute-start.7 = (f32[16,512]{1,0:T(8,128)S(1)}, f32[16,512]{1,0:T(8,128)S(1)}, u32[]{:S(2)}, u32[]{:S(2)}) collective-permute-start(f32[16,512]{1,0:T(8,128)S(1)} %copy-done.13), channel_id=1, source_target_pairs={{16,32},{32,16},{48,64},{64,48},{80,96},{96,80},{17,33},{33,17},{4... | collective-permute-start | bytes 98312 | tf_op jit(solution)/shard_map/ppermute | solution.py:539
  83.2 3.7 %collective-permute-start.4 = (f32[16,256]{1,0:T(8,128)S(1)}, f32[16,256]{1,0:T(8,128)S(1)}, u32[]{:S(2)}, u32[]{:S(2)}) collective-permute-start(f32[16,256]{1,0:T(8,128)S(1)} %copy-done.15), channel_id=1, source_target_pairs={{0,1},{1,0},{2,3},{3,2},{4,5},{5,4},{6,7},{7,6},{8,9},{9,8},{10,11... | collective-permute-start | bytes 49160 | tf_op jit(solution)/shard_map/ppermute | solution.py:539
  86.9 2.8 %collective-permute-done.4.col_a = f32[16,256]{1,0:T(8,128)S(1)} collective-permute-done((f32[16,256]{1,0:T(8,128)S(1)}, f32[16,256]{1,0:T(8,128)S(1)}, u32[]{:S(2)}, u32[]{:S(2)}) %collective-permute-start.4) | collective-permute-done | bytes 16416 | tf_op jit(solution)/shard_map/ppermute | solution.py:539
  89.7 6.6 %all-to-all-done.2 = f32[128,13,1,128]{3,2,1,0:T(1,128)S(1)} async-done(((f32[128,13,1,128]{3,2,1,0:T(1,128)}), f32[128,13,1,128]{3,2,1,0:T(1,128)S(1)}, u32[]{:S(2)}, u32[]{:S(2)}) %all-to-all-start.2) | async-done | bytes 852000 | tf_op jit(solution)/shard_map/all_to_all | solution.py:532
  96.3 12.4 %pair.3.forces = f32[1536,128]{1,0:T(8,128)} custom-call(s32[1]{0:T(128)} %bitcast.1.used, s32[2,256]{1,0:T(2,128)S(1)} %bitcast.26, f32[1664,128]{1,0:T(8,128)S(1)} %bitcast.23, f32[16,256]{1,0:T(8,128)S(1)} %collective-permute-done.4.col_a, f32[16,256]{1,0:T(8,128)S(1)} %collective-permute-done.5.col_b, f32[16,512]{1,0:T(8,128)S(1)} %collective-permute-done.6.row_a, ...), custom_call_target="tpu_custom_call" | custom-call | flops 2000000000 | bytes 2000000 | tf_op jit(solution)/shard_map/pair/pallas_call | solution.py:424
  108.7 4.6 %all-to-all-start.3 = ((f32[128,3,4,128]{3,2,1,0:T(4,128)}), f32[128,3,4,128]{3,2,1,0:T(4,128)}, u32[]{:S(2)}, u32[]{:S(2)}) async-start(f32[128,3,4,128]{3,2,1,0:T(4,128)} %bitcast.19), calls=%async_computation.3 | async-start | bytes 1572864 | tf_op jit(solution)/shard_map/all_to_all | solution.py:532
  113.3 10.5 %stencil.3.base = f32[3,1024,128]{2,1,0:T(8,128)} custom-call(s32[10]{0:T(128)} %stack.67.flags, f32[3,256,512]{2,1,0:T(8,128)} %get-tuple-element.18.x, f32[3,256,512]{2,1,0:T(8,128)} %get-tuple-element.19.velocity, f32[256,512]{1,0:T(8,128)} %stiffness.3, f32[16,256]{1,0:T(8,128)} %copy-done.9, f32[16,256]{1,0:T(8,128)} %copy-done.8, f32[16,512]{1,0:T(8,128)} %copy-done.5, ...), custom_call_target="tpu_custom_call" | custom-call | flops 20000000 | bytes 6000000 | tf_op jit(solution)/shard_map/stencil/pallas_call | solution.py:266
  123.8 5.0 %all-to-all-done.3 = f32[128,3,4,128]{3,2,1,0:T(4,128)} async-done(((f32[128,3,4,128]{3,2,1,0:T(4,128)}), f32[128,3,4,128]{3,2,1,0:T(4,128)}, u32[]{:S(2)}, u32[]{:S(2)}) %all-to-all-start.3) | async-done | bytes 786464 | tf_op jit(solution)/shard_map/all_to_all | solution.py:532
  128.9 5.5 %advance.3 = (f32[3,256,512]{2,1,0:T(8,128)}, f32[3,256,512]{2,1,0:T(8,128)}) custom-call(s32[512]{0:T(512)} %shift-right-logical_add_fusion.route, f32[1536,128]{1,0:T(8,128)} %bitcast.20.returned, f32[3,1024,128]{2,1,0:T(8,128)} %stencil.3.base, f32[3,256,512]{2,1,0:T(8,128)} %get-tuple-element.18.x), custom_call_target="tpu_custom_call" | custom-call | flops 2000000 | bytes 8000000 | tf_op jit(solution)/shard_map/advance/pallas_call | solution.py:510
  (44 shorter events, 2.2 us)
Async XLA Ops:
  5.6 16.1 %copy-start.14 = (f32[16,512]{1,0:T(8,128)S(1)}, f32[16,512]{1,0:T(8,128)}, u32[]{:S(2)}) copy-start(f32[16,512]{1,0:T(8,128)} %get-tuple-element.14) | copy-start | bytes 98308
  5.6 20.1 %copy-start.10 = (s32[1,1,2,256]{3,2,1,0:T(2,128)S(1)}, s32[1,1,2,256]{3,2,1,0:T(2,128)}, u32[]{:S(2)}) copy-start(s32[1,1,2,256]{3,2,1,0:T(2,128)} %param.9) | copy-start | bytes 6148
  5.6 29.0 %all-to-all-start = ((f32[128,13,1,128]{3,2,1,0:T(1,128)}), f32[128,13,1,128]{3,2,1,0:T(1,128)S(1)}, u32[]{:S(2)}, u32[]{:S(2)}) async-start(f32[128,13,1,128]{3,2,1,0:T(1,128)} %bitcast.28), calls=%async_computation | async-start | bytes 1703936 | tf_op jit(solution)/shard_map/all_to_all | solution.py:532
  17.1 9.2 %collective-permute-start.1 = (f32[16,256]{1,0:T(8,128)S(1)}, f32[16,256]{1,0:T(8,128)S(1)}, u32[]{:S(2)}, u32[]{:S(2)}) collective-permute-start(f32[16,256]{1,0:T(8,128)S(1)} %copy-done.16), channel_id=1, source_target_pairs={{1,2},{2,1},{3,4},{4,3},{5,6},{6,5},{7,8},{8,7},{9,10},{10,9},{11,... | collective-permute-start | bytes 49160 | tf_op jit(solution)/shard_map/ppermute | solution.py:539
  17.8 10.2 %collective-permute-start = (f32[16,256]{1,0:T(8,128)S(1)}, f32[16,256]{1,0:T(8,128)S(1)}, u32[]{:S(2)}, u32[]{:S(2)}) collective-permute-start(f32[16,256]{1,0:T(8,128)S(1)} %copy-done.16), channel_id=1, source_target_pairs={{0,1},{1,0},{2,3},{3,2},{4,5},{5,4},{6,7},{7,6},{8,9},{9,8},{10,11... | collective-permute-start | bytes 49160 | tf_op jit(solution)/shard_map/ppermute | solution.py:539
  21.7 7.0 %collective-permute-start.3 = (f32[16,512]{1,0:T(8,128)S(1)}, f32[16,512]{1,0:T(8,128)S(1)}, u32[]{:S(2)}, u32[]{:S(2)}) collective-permute-start(f32[16,512]{1,0:T(8,128)S(1)} %copy-done.14), channel_id=1, source_target_pairs={{16,32},{32,16},{48,64},{64,48},{80,96},{96,80},{17,33},{33,17},{4... | collective-permute-start | bytes 98312 | tf_op jit(solution)/shard_map/ppermute | solution.py:539
  25.6 3.0 %collective-permute-start.2 = (f32[16,512]{1,0:T(8,128)S(1)}, f32[16,512]{1,0:T(8,128)S(1)}, u32[]{:S(2)}, u32[]{:S(2)}) collective-permute-start(f32[16,512]{1,0:T(8,128)S(1)} %copy-done.14), channel_id=1, source_target_pairs={{0,16},{16,0},{32,48},{48,32},{64,80},{80,64},{96,112},{112,96},{1... | collective-permute-start | bytes 98312 | tf_op jit(solution)/shard_map/ppermute | solution.py:539
  26.3 20.5 %copy-start.6 = (f32[16,256]{1,0:T(8,128)}, f32[16,256]{1,0:T(8,128)S(1)}, u32[]{:S(2)}) copy-start(f32[16,256]{1,0:T(8,128)S(1)} %collective-permute-done.1.col_b) | copy-start | bytes 49156
  28.0 18.9 %copy-start.7 = (f32[16,256]{1,0:T(8,128)}, f32[16,256]{1,0:T(8,128)S(1)}, u32[]{:S(2)}) copy-start(f32[16,256]{1,0:T(8,128)S(1)} %collective-permute-done.col_a) | copy-start | bytes 49156
  28.6 18.2 %copy-start.2 = (f32[16,512]{1,0:T(8,128)}, f32[16,512]{1,0:T(8,128)S(1)}, u32[]{:S(2)}) copy-start(f32[16,512]{1,0:T(8,128)S(1)} %collective-permute-done.3.row_b) | copy-start | bytes 98308
  28.6 18.2 %copy-start.3 = (f32[16,512]{1,0:T(8,128)}, f32[16,512]{1,0:T(8,128)S(1)}, u32[]{:S(2)}) copy-start(f32[16,512]{1,0:T(8,128)S(1)} %collective-permute-done.2.row_a) | copy-start | bytes 98308
  46.9 20.2 %all-to-all-start.1 = ((f32[128,3,4,128]{3,2,1,0:T(4,128)}), f32[128,3,4,128]{3,2,1,0:T(4,128)}, u32[]{:S(2)}, u32[]{:S(2)}) async-start(f32[128,3,4,128]{3,2,1,0:T(4,128)} %bitcast.5), calls=%async_computation.1 | async-start | bytes 1572864 | tf_op jit(solution)/shard_map/all_to_all | solution.py:532
  74.0 22.3 %copy-start.11 = (s32[1,1,2,256]{3,2,1,0:T(2,128)S(1)}, s32[1,1,2,256]{3,2,1,0:T(2,128)}, u32[]{:S(2)}) copy-start(s32[1,1,2,256]{3,2,1,0:T(2,128)} %param.9) | copy-start | bytes 6148
  74.0 22.3 %all-to-all-start.2 = ((f32[128,13,1,128]{3,2,1,0:T(1,128)}), f32[128,13,1,128]{3,2,1,0:T(1,128)S(1)}, u32[]{:S(2)}, u32[]{:S(2)}) async-start(f32[128,13,1,128]{3,2,1,0:T(1,128)} %bitcast.27), calls=%async_computation.2 | async-start | bytes 1703936 | tf_op jit(solution)/shard_map/all_to_all | solution.py:532
  78.8 10.8 %collective-permute-start.7 = (f32[16,512]{1,0:T(8,128)S(1)}, f32[16,512]{1,0:T(8,128)S(1)}, u32[]{:S(2)}, u32[]{:S(2)}) collective-permute-start(f32[16,512]{1,0:T(8,128)S(1)} %copy-done.13), channel_id=1, source_target_pairs={{16,32},{32,16},{48,64},{64,48},{80,96},{96,80},{17,33},{33,17},{4... | collective-permute-start | bytes 98312 | tf_op jit(solution)/shard_map/ppermute | solution.py:539
  82.4 7.3 %collective-permute-start.6 = (f32[16,512]{1,0:T(8,128)S(1)}, f32[16,512]{1,0:T(8,128)S(1)}, u32[]{:S(2)}, u32[]{:S(2)}) collective-permute-start(f32[16,512]{1,0:T(8,128)S(1)} %copy-done.13), channel_id=1, source_target_pairs={{0,16},{16,0},{32,48},{48,32},{64,80},{80,64},{96,112},{112,96},{1... | collective-permute-start | bytes 98312 | tf_op jit(solution)/shard_map/ppermute | solution.py:539
  82.5 4.4 %collective-permute-start.5 = (f32[16,256]{1,0:T(8,128)S(1)}, f32[16,256]{1,0:T(8,128)S(1)}, u32[]{:S(2)}, u32[]{:S(2)}) collective-permute-start(f32[16,256]{1,0:T(8,128)S(1)} %copy-done.15), channel_id=1, source_target_pairs={{1,2},{2,1},{3,4},{4,3},{5,6},{6,5},{7,8},{8,7},{9,10},{10,9},{11,... | collective-permute-start | bytes 49160 | tf_op jit(solution)/shard_map/ppermute | solution.py:539
  83.2 6.5 %collective-permute-start.4 = (f32[16,256]{1,0:T(8,128)S(1)}, f32[16,256]{1,0:T(8,128)S(1)}, u32[]{:S(2)}, u32[]{:S(2)}) collective-permute-start(f32[16,256]{1,0:T(8,128)S(1)} %copy-done.15), channel_id=1, source_target_pairs={{0,1},{1,0},{2,3},{3,2},{4,5},{5,4},{6,7},{7,6},{8,9},{9,8},{10,11... | collective-permute-start | bytes 49160 | tf_op jit(solution)/shard_map/ppermute | solution.py:539
  86.9 21.8 %copy-start.8 = (f32[16,256]{1,0:T(8,128)}, f32[16,256]{1,0:T(8,128)S(1)}, u32[]{:S(2)}) copy-start(f32[16,256]{1,0:T(8,128)S(1)} %collective-permute-done.5.col_b) | copy-start | bytes 49156
  89.7 19.0 %copy-start.9 = (f32[16,256]{1,0:T(8,128)}, f32[16,256]{1,0:T(8,128)S(1)}, u32[]{:S(2)}) copy-start(f32[16,256]{1,0:T(8,128)S(1)} %collective-permute-done.4.col_a) | copy-start | bytes 49156
  89.7 19.0 %copy-start.4 = (f32[16,512]{1,0:T(8,128)}, f32[16,512]{1,0:T(8,128)S(1)}, u32[]{:S(2)}) copy-start(f32[16,512]{1,0:T(8,128)S(1)} %collective-permute-done.7.row_b) | copy-start | bytes 98308
  89.7 19.0 %copy-start.5 = (f32[16,512]{1,0:T(8,128)}, f32[16,512]{1,0:T(8,128)S(1)}, u32[]{:S(2)}) copy-start(f32[16,512]{1,0:T(8,128)S(1)} %collective-permute-done.6.row_a) | copy-start | bytes 98308
  96.3 12.4 %copy-start.1 = (f32[128,13,1,128]{3,2,1,0:T(1,128)}, f32[128,13,1,128]{3,2,1,0:T(1,128)S(1)}, u32[]{:S(2)}) copy-start(f32[128,13,1,128]{3,2,1,0:T(1,128)S(1)} %all-to-all-done.2) | copy-start | bytes 2555908
  108.7 20.2 %all-to-all-start.3 = ((f32[128,3,4,128]{3,2,1,0:T(4,128)}), f32[128,3,4,128]{3,2,1,0:T(4,128)}, u32[]{:S(2)}, u32[]{:S(2)}) async-start(f32[128,3,4,128]{3,2,1,0:T(4,128)} %bitcast.19), calls=%async_computation.3 | async-start | bytes 1572864 | tf_op jit(solution)/shard_map/all_to_all | solution.py:532
  (5 other events, 42.6 us)
